TPU v7x, 512 devices: a whole 4x8x8 slice. The times are simulated.
512 devices in a mesh: member: 16 (over z, core), band: 32 (over y, x).
Axes of the slice: x: 4, y: 8, z: 8, core: 2. Of those that a mesh axis runs over, the one named last changes fastest.
Arguments:
- ensemble: bfloat16 [16, 2, 16, 128, 1440], P('member', None, None, 'band'), may hold values from -6 to 6
- member_weight: float32 [16], replicated, may hold values from 0.5 to 2
- member_of_slot: int32 [16], P('member'), may hold values from 0 to 15, each once
- halfwidth: int32 [16], replicated, may hold values from 1 to 4, as said below
- static_root: float32 [16, 16], replicated, may hold values from -1.5 to 1.5
- innovation: bfloat16 [2, 16, 128, 1440], P(None, None, 'band'), may hold values from -6 to 6
- precision: bfloat16 [16, 128, 1440], P(None, 'band'), may hold values from 0.1 to 3
Outputs:
- control_members: float32 [16, 16, 128, 1440], P('member', None, 'band')
- control_static: float32 [16, 128, 1440], P(None, 'band')
- increment: float32 [2, 16, 128, 1440], P(None, 'member', 'band')
Inputs may be any that keep to these rules, and one draw needn't show every extreme that they name: `member_of_slot`: each member appears in exactly one slot. `halfwidth`: some level has a half-width of exactly 4.
All inputs are finite; a program needn't handle non-finite values.
Results may differ from a plain program's by a relative error of at most 0.0062.
Values may be sent and summed in bfloat16 or wider, within the bound.
A program may use at most 64 MiB of HBM per device.

v0:
```python
import math

import jax
import jax.numpy as jnp
from jax import lax
from jax.sharding import PartitionSpec as P

ITERS = 2
HMAX = 4
LREACH = 18


ensemble_share = 0.8
static_share = 0.6
length_scale = 6.0


def with_halo(block, sides, width):
    for axis, dim in sides:
        count = lax.axis_size(axis)
        forward = [(i, i + 1) for i in range(count - 1)]
        backward = [(target, source) for source, target in forward]
        low = lax.ppermute(
            lax.slice_in_dim(block, block.shape[dim] - width, None, axis=dim), axis, forward
        )
        high = lax.ppermute(lax.slice_in_dim(block, 0, width, axis=dim), axis, backward)
        block = jnp.concatenate([low, block, high], axis=dim)
    return block


def lon_kernel(reach, width):
    rows_index = jnp.arange(width + 2 * reach, dtype=jnp.int32)[:, None]
    cols_index = jnp.arange(width, dtype=jnp.int32)[None, :]
    distance = jnp.abs(rows_index - reach - cols_index).astype(jnp.float32)
    values = jnp.exp(-0.5 * (distance / length_scale) ** 2) / (
        length_scale * math.sqrt(2.0 * math.pi)
    )
    return jnp.where(distance <= reach, values, jnp.zeros_like(values)).astype(jnp.bfloat16)


def smooth_longitude(field, reach, blocks):
    width = field.shape[-1] // blocks
    pieces = field.reshape(field.shape[:-1] + (blocks, width))
    before = jnp.roll(pieces, 1, axis=-2)[..., width - reach :]
    after = jnp.roll(pieces, -1, axis=-2)[..., :reach]
    window = jnp.concatenate([before, pieces, after], axis=-1)
    kernel = lon_kernel(reach, width)
    result = jnp.einsum("...bm,mo->...bo", window, kernel, preferred_element_type=jnp.float32)
    return result.reshape(field.shape).astype(jnp.bfloat16)


def taper_weights(halfwidth, reach):
    offsets = jnp.abs(jnp.arange(-reach, reach + 1, dtype=jnp.int32)).astype(jnp.float32)
    spans = halfwidth.astype(jnp.float32)[:, None] + 1.0
    return jnp.maximum(1.0 - offsets[None, :] / spans, 0.0) / spans


def localize(field, taper):
    smoothed = smooth_longitude(field.astype(jnp.bfloat16), LREACH, 3)
    padded = with_halo(smoothed, (("band", 2),), HMAX)
    row_count = field.shape[2]
    summed = jnp.zeros(field.shape, jnp.float32)
    for offset in range(2 * HMAX + 1):
        summed = summed + taper[:, offset][None, :, None, None] * padded[
            :, :, offset : offset + row_count, :
        ].astype(jnp.float32)
    return summed


def local_dot(first_members, second_members, first_static, second_static, groups):
    return jnp.sum(first_members * second_members) + jnp.sum(first_static * second_static) / groups


def shards(ensemble, member_weight, member_of_slot, halfwidth, static_root, innovation, precision):
    member_count = member_weight.shape[0]
    picker = (member_of_slot[:, None] == jnp.arange(member_count, dtype=jnp.int32)[None, :]).astype(
        jnp.float32
    )
    scaled = jnp.sum(picker * member_weight[None, :], axis=1)
    taper = taper_weights(halfwidth, HMAX)
    precise = precision.astype(jnp.float32)
    groups = lax.axis_size("member")
    level_share = precision.shape[0] // groups
    first_level = lax.axis_index("member") * level_share

    def adjoint(weighted):
        folded = scaled[:, None, None, None] * jnp.sum(
            ensemble.astype(jnp.float32) * weighted[None], axis=1
        )
        grad_members = ensemble_share * localize(folded, taper)
        grad_static = static_share * jnp.einsum(
            "ql,qyx->lyx", static_root, jnp.sum(weighted, axis=0), precision=lax.Precision.HIGHEST
        )
        return (grad_members, grad_static)

    res_members, res_static = adjoint(precise[None] * innovation.astype(jnp.float32))
    dir_members, dir_static = (res_members, res_static)
    sol_members = jnp.zeros_like(res_members)
    sol_static = jnp.zeros_like(res_static)
    increment = jnp.zeros((), jnp.float32)
    norm_now = lax.psum(
        local_dot(res_members, res_members, res_static, res_static, groups), ("member", "band")
    )
    for iteration in range(ITERS):
        localized = localize(dir_members, taper)
        partial_image = ensemble_share * jnp.sum(
            scaled[:, None, None, None, None] * ensemble.astype(jnp.float32) * localized[:, None],
            axis=0,
        )
        summed = lax.psum(partial_image, "member")
        static = jnp.einsum("lq,qyx->lyx", static_root, dir_static, precision=lax.Precision.HIGHEST)
        image = summed + static_share * static[None]
        hessian_weighted = precise[None] * image
        hessian_grad_members, hessian_grad_static = adjoint(hessian_weighted)
        hes_members, hes_static, image = (
            dir_members + hessian_grad_members,
            dir_static + hessian_grad_static,
            image,
        )
        curvature = lax.psum(
            local_dot(dir_members, hes_members, dir_static, hes_static, groups), ("member", "band")
        )
        alpha = norm_now / curvature
        sol_members = sol_members + alpha * dir_members
        sol_static = sol_static + alpha * dir_static
        increment = increment + alpha * image
        res_members = res_members - alpha * hes_members
        res_static = res_static - alpha * hes_static
        if iteration + 1 < ITERS:
            norm_next = lax.psum(
                local_dot(res_members, res_members, res_static, res_static, groups),
                ("member", "band"),
            )
            ratio = norm_next / norm_now
            dir_members = res_members + ratio * dir_members
            dir_static = res_static + ratio * dir_static
            norm_now = norm_next
    increment = lax.dynamic_slice_in_dim(increment, first_level, level_share, 1)
    return (sol_members, sol_static, increment)


def solution(mesh):
    return jax.shard_map(
        shards,
        mesh=mesh,
        in_specs=(
            P("member", None, None, "band", None),
            P(),
            P("member"),
            P(),
            P(),
            P(None, None, "band", None),
            P(None, "band", None),
        ),
        out_specs=(
            P("member", None, "band", None),
            P(None, "band", None),
            P(None, "member", "band", None),
        ),
        check_vma=False,
    )
```

profile of v0, /device:TPU:1, one launch (start us, length us, event | category | flops | bytes accessed | tf_op | source)
XLA Modules:
  0.0 658.5 jit_solution(16516160532751708579)
XLA Ops:
  8.9 1.3 fusion.100
  10.1 1.6 fusion.13
  14.2 4.0 collective-permute-start
  18.2 1.3 collective-permute-start.1
  20.8 3.8 collective-permute-done.1
  26.7 4.0 collective-permute-start.2
  31.0 1.3 collective-permute-start.3
  33.3 4.1 collective-permute-done.3
  38.1 1.8 fusion.10
  41.3 126.7 %all-reduce.4.cloned.1.call-done = f32[2,16,4,1440]{3,2,1,0:T(4,128)} async-done(((f32[2,16,4,1440]{3,2,1,0:T(4,128)}), f32[2,16,4,1440]{3,2,1,0:T(4,128)}) %all-reduce.4.cloned.1.call-update) | async-done | bytes 737296 | tf_op jit(solution)/shard_map/psum | solution.py:110
  168.0 1.7 multiply_reduce_fusion.1
  172.6 3.1 collective-permute-start.4
  175.7 1.3 collective-permute-start.5
  177.0 1.4 fusion.42
  179.7 3.3 collective-permute-done.5
  184.0 2.1 multiply_reduce_fusion.4
  187.4 101.5 %all-reduce = (f32[]{:T(128)}, f32[]{:T(128)}) all-reduce(f32[]{:T(128)S(6)} %add.217, f32[]{:T(128)S(6)} %add.238), channel_id=1, replica_groups=mesh['member'=16,'band'=32] {'member','band'}, use_global_device_ids=true, to_apply=%region_5.6 | all-reduce | flops 2 | bytes 16 | tf_op jit(solution)/shard_map/psum | solution.py:101
  292.7 94.9 %psum.45 = f32[]{:T(128)} all-reduce(f32[]{:T(128)S(6)} %add.239), channel_id=1, replica_groups=mesh['member'=16,'band'=32] {'member','band'}, use_global_device_ids=true, to_apply=%region_14.15 | all-reduce | flops 1 | bytes 8 | tf_op jit(solution)/shard_map/psum | solution.py:130
  394.0 3.7 collective-permute-start.6
  397.7 1.3 collective-permute-start.7
  399.0 2.2 collective-permute-done.6
  401.3 3.8 collective-permute-done.7
  405.8 1.8 fusion.12
  409.1 116.4 %all-reduce.6.cloned.1.call-done = f32[2,16,4,1440]{3,2,1,0:T(4,128)} async-done(((f32[2,16,4,1440]{3,2,1,0:T(4,128)}), f32[2,16,4,1440]{3,2,1,0:T(4,128)}) %all-reduce.6.cloned.1.call-update) | async-done | bytes 737296 | tf_op jit(solution)/shard_map/psum | solution.py:110
  525.5 1.8 multiply_reduce_fusion
  531.2 3.1 collective-permute-start.8
  534.3 1.3 collective-permute-start.9
  535.6 1.2 fusion.17
  537.8 3.9 collective-permute-done.9
  542.7 2.0 fusion.39
  545.3 101.3 %psum.47 = f32[]{:T(128)} all-reduce(f32[]{:T(128)S(6)} %add.262), channel_id=1, replica_groups=mesh['member'=16,'band'=32] {'member','band'}, use_global_device_ids=true, to_apply=%region_20.21 | all-reduce | flops 1 | bytes 8 | tf_op jit(solution)/shard_map/psum | solution.py:120
  647.9 1.4 fusion.92
  (145 shorter events, 29.7 us)
Async XLA Ops:
  7.2 32.8 %copy-start = (f32[16,16]{1,0:T(8,128)S(1)}, f32[16,16]{1,0:T(8,128)}, u32[]{:S(2)}) copy-start(f32[16,16]{1,0:T(8,128)} %param.11) | copy-start | bytes 3076
  7.2 160.8 %all-reduce.4.cloned.1.call-start = ((), (), s32[]{:S(2)}) async-start(), calls=%async_computation | async-start | bytes 1572864 | tf_op jit(solution)/shard_map/psum | solution.py:110
  12.9 158.4 %copy-start.25 = (s32[516]{0:T(1024)}, s32[516]{0:T(1024)S(1)}, u32[]{:S(2)}) copy-start(s32[516]{0:T(1024)S(1)} %iota_add_fusion) | copy-start | bytes 6196
  14.2 6.6 collective-permute-start
  18.2 6.4 collective-permute-start.1
  19.6 17.9 %copy-start.4 = (f32[16]{0:T(128)}, f32[16]{0:T(128)S(1)}, u32[]{:S(2)}) copy-start(f32[16]{0:T(128)S(1)} %get-tuple-element.60) | copy-start | bytes 196
  19.6 17.9 %copy-start.7 = (f32[16]{0:T(128)}, f32[16]{0:T(128)S(1)}, u32[]{:S(2)}) copy-start(f32[16]{0:T(128)S(1)} %get-tuple-element.61) | copy-start | bytes 196
  19.6 17.9 %copy-start.10 = (f32[16]{0:T(128)}, f32[16]{0:T(128)S(1)}, u32[]{:S(2)}) copy-start(f32[16]{0:T(128)S(1)} %get-tuple-element.62) | copy-start | bytes 196
  19.6 17.9 %copy-start.13 = (f32[16]{0:T(128)}, f32[16]{0:T(128)S(1)}, u32[]{:S(2)}) copy-start(f32[16]{0:T(128)S(1)} %get-tuple-element.63) | copy-start | bytes 196
  19.6 17.9 %copy-start.16 = (f32[16]{0:T(128)}, f32[16]{0:T(128)S(1)}, u32[]{:S(2)}) copy-start(f32[16]{0:T(128)S(1)} %get-tuple-element.64) | copy-start | bytes 196
  19.6 17.9 %copy-start.19 = (f32[16]{0:T(128)}, f32[16]{0:T(128)S(1)}, u32[]{:S(2)}) copy-start(f32[16]{0:T(128)S(1)} %get-tuple-element.65) | copy-start | bytes 196
  19.6 17.9 %copy-start.22 = (f32[16]{0:T(128)}, f32[16]{0:T(128)S(1)}, u32[]{:S(2)}) copy-start(f32[16]{0:T(128)S(1)} %get-tuple-element.66) | copy-start | bytes 196
  26.7 6.6 %collective-permute-start.2 = (bf16[1,16,4,1440]{3,1,2,0:T(8,128)(2,1)S(1)}, bf16[1,16,4,1440]{3,1,2,0:T(8,128)(2,1)S(1)}, u32[]{:S(2)}, u32[]{:S(2)}) collective-permute-start(bf16[1,16,4,1440]{3,1,2,0:T(8,128)(2,1)S(1)} %convert_element_type.392), channel_id=1, source_target_pairs={{0,1},{1,2},{2,3},{3,4},{4,5},{5,6},{6,7},{7,8},{8,9},{9,10},{10,1... | collective-permute-start | bytes 552968 | tf_op jit(solution)/shard_map/ppermute | solution.py:23
  31.0 6.4 collective-permute-start.3
  39.9 485.6 %all-reduce.6.cloned.1.call-start = ((), (), s32[]{:S(2)}) async-start(), calls=%async_computation.1 | async-start | bytes 1572864 | tf_op jit(solution)/shard_map/psum | solution.py:110
  172.6 7.1 %collective-permute-start.4 = (bf16[1,16,4,1440]{3,1,2,0:T(8,128)(2,1)S(1)}, bf16[1,16,4,1440]{3,1,2,0:T(8,128)(2,1)S(1)}, u32[]{:S(2)}, u32[]{:S(2)}) collective-permute-start(bf16[1,16,4,1440]{3,1,2,0:T(8,128)(2,1)S(1)} %convert_element_type.405), channel_id=1, source_target_pairs={{0,1},{1,2},{2,3},{3,4},{4,5},{5,6},{6,7},{7,8},{8,9},{9,10},{10,1... | collective-permute-start | bytes 552968 | tf_op jit(solution)/shard_map/ppermute | solution.py:23
  175.7 7.3 %collective-permute-start.5 = (bf16[1,16,4,1440]{3,1,2,0:T(8,128)(2,1)S(1)}, bf16[1,16,4,1440]{3,1,2,0:T(8,128)(2,1)}, u32[]{:S(2)}, u32[]{:S(2)}) collective-permute-start(bf16[1,16,4,1440]{3,1,2,0:T(8,128)(2,1)S(1)} %convert_element_type.405), channel_id=1, source_target_pairs={{1,0},{2,1},{3,2},{4,3},{5,4},{6,5},{7,6},{8,7},{9,8},{10,9},{11,1... | collective-permute-start | bytes 552968 | tf_op jit(solution)/shard_map/ppermute | solution.py:26
  394.0 11.1 %copy-start.5 = (f32[16]{0:T(128)S(1)}, f32[16]{0:T(128)}, u32[]{:S(2)}) copy-start(f32[16]{0:T(128)} %copy-done.4) | copy-start | bytes 196
  394.0 11.1 %copy-start.8 = (f32[16]{0:T(128)S(1)}, f32[16]{0:T(128)}, u32[]{:S(2)}) copy-start(f32[16]{0:T(128)} %copy-done.7) | copy-start | bytes 196
  394.0 11.1 %copy-start.11 = (f32[16]{0:T(128)S(1)}, f32[16]{0:T(128)}, u32[]{:S(2)}) copy-start(f32[16]{0:T(128)} %copy-done.10) | copy-start | bytes 196
  394.0 11.1 %copy-start.14 = (f32[16]{0:T(128)S(1)}, f32[16]{0:T(128)}, u32[]{:S(2)}) copy-start(f32[16]{0:T(128)} %copy-done.13) | copy-start | bytes 196
  394.0 11.1 %copy-start.17 = (f32[16]{0:T(128)S(1)}, f32[16]{0:T(128)}, u32[]{:S(2)}) copy-start(f32[16]{0:T(128)} %copy-done.16) | copy-start | bytes 196
  394.0 11.1 %copy-start.20 = (f32[16]{0:T(128)S(1)}, f32[16]{0:T(128)}, u32[]{:S(2)}) copy-start(f32[16]{0:T(128)} %copy-done.19) | copy-start | bytes 196
  394.0 11.1 %copy-start.23 = (f32[16]{0:T(128)S(1)}, f32[16]{0:T(128)}, u32[]{:S(2)}) copy-start(f32[16]{0:T(128)} %copy-done.22) | copy-start | bytes 196
  394.0 7.2 %collective-permute-start.6 = (bf16[1,16,4,1440]{3,1,2,0:T(8,128)(2,1)S(1)}, bf16[1,16,4,1440]{3,1,2,0:T(8,128)(2,1)S(1)}, u32[]{:S(2)}, u32[]{:S(2)}) collective-permute-start(bf16[1,16,4,1440]{3,1,2,0:T(8,128)(2,1)S(1)} %convert_element_type.417), channel_id=1, source_target_pairs={{0,1},{1,2},{2,3},{3,4},{4,5},{5,6},{6,7},{7,8},{8,9},{9,10},{10,1... | collective-permute-start | bytes 552968 | tf_op jit(solution)/shard_map/ppermute | solution.py:23
  397.7 7.4 %collective-permute-start.7 = (bf16[1,16,4,1440]{3,1,2,0:T(8,128)(2,1)S(1)}, bf16[1,16,4,1440]{3,1,2,0:T(8,128)(2,1)S(1)}, u32[]{:S(2)}, u32[]{:S(2)}) collective-permute-start(bf16[1,16,4,1440]{3,1,2,0:T(8,128)(2,1)S(1)} %convert_element_type.417), channel_id=1, source_target_pairs={{1,0},{2,1},{3,2},{4,3},{5,4},{6,5},{7,6},{8,7},{9,8},{10,9},{11,1... | collective-permute-start | bytes 552968 | tf_op jit(solution)/shard_map/ppermute | solution.py:26
  531.2 6.5 collective-permute-start.8
  534.3 7.3 %collective-permute-start.9 = (bf16[1,16,4,1440]{3,1,2,0:T(8,128)(2,1)S(1)}, bf16[1,16,4,1440]{3,1,2,0:T(8,128)(2,1)}, u32[]{:S(2)}, u32[]{:S(2)}) collective-permute-start(bf16[1,16,4,1440]{3,1,2,0:T(8,128)(2,1)S(1)} %convert_element_type.430), channel_id=1, source_target_pairs={{1,0},{2,1},{3,2},{4,3},{5,4},{6,5},{7,6},{8,7},{9,8},{10,9},{11,1... | collective-permute-start | bytes 552968 | tf_op jit(solution)/shard_map/ppermute | solution.py:26
  536.9 5.8 copy-start.15
  536.9 5.8 copy-start.18
  536.9 5.8 copy-start.21
  536.9 5.8 copy-start.24
  (9 other events, 33.3 us)
Sparse Core Ops, SparseCore 0:
  40.1 127.9 all-reduce.3
  407.7 117.7 all-reduce.5
where the time goes:
time: 659 us; the launch traced here: 658 us
  blocking collectives  298 us (45%)
  waiting for transfers between devices  266 us (40%)
  between operations  24.5 us (4%)
  starting transfers between devices  24.4 us (4%)
  other arithmetic  23.4 us (4%)
  local copies, waits for them, and re-layouts  13.4 us (2%)
  matrix products  8.49 us (1%)
    psum x2, waiting for transfers between devices, shards(): summed = lax.psum(partial_image, 'member')  243 us
    psum x2, blocking collectives, shards(): lax.psum(local_dot(res_members, res_members, res_static, res_static, grou...  196 us
    psum x1, blocking collectives, shards(): lax.psum(local_dot(dir_members, hes_members, dir_static, hes_static, grou...  101 us
    ppermute x5, waiting for transfers between devices, with_halo(): lax.ppermute(lax.slice_in_dim(block, 0, width, axis=dim), axis, backward)  18.7 us
    ppermute x5, starting transfers between devices, with_halo(): lax.ppermute(lax.slice_in_dim(block, block.shape[dim] - width, None, axis...  17.9 us
  transfers between devices with their start and end apart: 12, of which 11 were waited for; matrix products, arithmetic and copies ran while one was open for 1% of the time, Pallas kernels for 0%

commit v1 on v0

v1 whole, which is shorter than its diff:
```python
import functools
import math

import jax
import jax.numpy as jnp
import numpy as np
from jax import lax
from jax.experimental import pallas as pl
from jax.experimental.pallas import tpu as pltpu
from jax.sharding import PartitionSpec as P

HMAX = 4
LREACH = 18
TILE = 256
EDGE = 128

ensemble_share = 0.8
static_share = 0.6
length_scale = 6.0
MESH = pl.DeviceIdType.MESH


def window_weights(width, padded):
    tiles = padded // TILE
    kinds = []
    for tile in (0, 1, tiles - 1):
        start = tile * TILE
        rows = np.arange(start - EDGE, start + TILE + EDGE)
        if tile == 0:
            rows[:EDGE] = np.arange(padded - EDGE, padded)
        if tile == tiles - 1:
            rows[-EDGE:] = np.arange(EDGE)
        cols = np.arange(start, start + TILE)
        apart = np.abs(rows[:, None] - cols[None, :])
        apart = np.minimum(apart, width - apart)
        near = (apart <= LREACH) & (rows[:, None] < width) & (cols[None, :] < width)
        distance = apart.astype(np.float32)
        values = np.exp(-0.5 * (distance / np.float32(length_scale)) ** 2) / np.float32(
            length_scale * math.sqrt(2.0 * math.pi)
        )
        kinds.append(np.where(near, values, 0.0).astype(np.float32))
    return np.stack(kinds)


def halves(matrix):
    high = lax.reduce_precision(matrix, 8, 7)
    return jnp.stack([high, matrix - high]).astype(jnp.bfloat16)


def mul(a, b):
    return jnp.dot(a, b, preferred_element_type=jnp.float32)


def mul_wide(weights, field):
    high = field.astype(jnp.bfloat16)
    low = (field - high.astype(jnp.float32)).astype(jnp.bfloat16)
    return mul(weights[0], high) + mul(weights[0], low) + mul(weights[1], high)


def kernel(
    members, bands, across, tiles,
    ens_ref, w0_ref, p_ref, t1_ref, t2_ref, c1_ref, c2_ref, sel_ref, krt_ref, krm_ref, wk_ref,
    outm_ref, outs_ref, inc_ref,
    x_ref, s_ref, hp_ref, hn_ref, part_ref, rs_ref, gown_ref, gall_ref,
    r0_ref, r1_ref, r0s_ref, r1s_ref, im0_ref, im1_ref,
    vec_ref, tot_ref, allm_ref, allx_ref, ally_ref,
    h_send, h_recv, rs_send, rs_recv, g_send, g_recv, m_send, m_recv, x_send, x_recv, y_send, y_recv,
):
    m = lax.axis_index("member")
    band = lax.axis_index("band")
    up = bands // across
    by = band // across
    bx = lax.rem(band, across)
    levels = gall_ref.shape[0]
    eight = gall_ref.shape[1]
    rows2 = levels * eight
    rows1 = rows2 // 2

    def at_m(o):
        return lax.rem(m + o, members)

    def at_band(o):
        return lax.rem(band + o, bands)

    def x_peer(o):
        return lax.rem(bx + o, across)

    def y_peer(o):
        return lax.rem(by + o, up)

    barrier = pltpu.get_barrier_semaphore()
    greeted = 0
    for o in range(1, members):
        pl.semaphore_signal(
            barrier, inc=1, device_id=(at_m(o), band), device_id_type=MESH
        )
        greeted += 1
    others = [at_band(1), at_band(bands - 1)]
    others += [by * across + x_peer(o) for o in range(1, across)]
    others += [y_peer(o) * across + bx for o in range(1, up)]
    for other in others:
        pl.semaphore_signal(barrier, inc=1, device_id=(m, other), device_id_type=MESH)
        greeted += 1
    pl.semaphore_wait(barrier, greeted)

    sends = []

    def push(src, dst, send, recv, member, other):
        copy = pltpu.make_async_remote_copy(
            src_ref=src, dst_ref=dst, send_sem=send, recv_sem=recv,
            device_id=(member, other), device_id_type=MESH,
        )
        copy.start()
        sends.append(copy)
        return copy

    def arrived(like, dst, send, recv, member, other):
        pltpu.make_async_remote_copy(
            src_ref=like, dst_ref=dst, send_sem=send, recv_sem=recv,
            device_id=(member, other), device_id_type=MESH,
        ).wait_recv()

    def columns(i):
        return pl.ds(pl.multiple_of(i * TILE, TILE), TILE)

    def over_tiles(body, init=None):
        if init is None:
            def step(i, carry):
                body(columns(i))
                return carry
            lax.fori_loop(0, tiles, step, 0)
            return None
        return lax.fori_loop(0, tiles, lambda i, carry: body(columns(i), carry), init)

    def smooth(phase):
        out = s_ref.at[phase]
        last = tiles * TILE
        first = jnp.concatenate(
            [x_ref[:, last - EDGE : last], x_ref[:, : TILE + EDGE]], axis=1
        )
        out[:, :TILE] = mul(first, wk_ref[0]).astype(jnp.bfloat16)

        def inner(i, carry):
            start = pl.multiple_of(i * TILE - EDGE, EDGE)
            window = x_ref[:, pl.ds(start, TILE + 2 * EDGE)]
            out[:, columns(i)] = mul(window, wk_ref[1]).astype(jnp.bfloat16)
            return carry

        lax.fori_loop(1, tiles - 1, inner, 0)
        final = jnp.concatenate(
            [x_ref[:, last - TILE - EDGE : last], x_ref[:, :EDGE]], axis=1
        )
        out[:, last - TILE : last] = mul(final, wk_ref[2]).astype(jnp.bfloat16)

    def send_halo(phase):
        up_copy = push(
            s_ref.at[phase], hp_ref.at[phase], h_send.at[phase, 0], h_recv.at[phase, 0],
            m, at_band(1),
        )
        down_copy = push(
            s_ref.at[phase], hn_ref.at[phase], h_send.at[phase, 1], h_recv.at[phase, 1],
            m, at_band(bands - 1),
        )
        return up_copy, down_copy

    def stacked(phase, cols):
        return jnp.concatenate(
            [hp_ref[phase, :, cols], s_ref[phase, :, cols], hn_ref[phase, :, cols]], axis=0
        )

    def fold(cols, field):
        products = (ens_ref[:, cols] * field).reshape(levels, eight, TILE)
        both = (products + pltpu.roll(products, eight // 2, 1)).reshape(rows2, TILE)
        x_ref[:, cols] = mul(sel_ref[...], both.astype(jnp.bfloat16)).astype(jnp.bfloat16)

    def image(phase, stage, static_ref, out):
        def partial(cols):
            localized = mul(t2_ref[...], stacked(phase, cols)) * c2_ref[...]
            products = (localized * ens_ref[:, cols]).reshape(levels, eight, TILE)
            part_ref[stage, :, :, cols] = products.astype(jnp.bfloat16)

        over_tiles(partial)
        copies = []
        for o in range(1, members):
            copies.append(push(
                part_ref.at[stage, at_m(o)], rs_ref.at[stage, o - 1],
                rs_send.at[stage, o - 1], rs_recv.at[stage, o - 1], at_m(o), band,
            ))

        def static(cols):
            out[:, cols] = static_share * mul_wide(krm_ref, static_ref[:, cols])

        over_tiles(static)
        for copy in copies:
            copy.wait_recv()

        def collect(cols):
            out[:, cols] = (
                out[:, cols]
                + part_ref[stage, m, :, cols].astype(jnp.float32)
                + jnp.sum(rs_ref[stage, :, :, cols].astype(jnp.float32), axis=0)
            )

        over_tiles(collect)

    def squares(a, b):
        return jnp.sum((a * b).reshape(rows1 // 8, 8, TILE), axis=0)

    def total_of(acc):
        return jnp.sum(jnp.sum(acc, axis=1, keepdims=True), axis=0, keepdims=True)

    def pack(values):
        row = lax.broadcasted_iota(jnp.int32, (8, 128), 0)
        packed = jnp.zeros((8, 128), jnp.float32)
        for at, value in enumerate(values):
            packed = jnp.where(row == at, value, packed)
        return packed

    def gather_start(k, stage, value, table, count, own, peer, send, recv):
        vec_ref[k, stage] = value
        table[k, own] = value
        for o in range(1, count):
            member, other = peer(o)
            push(
                vec_ref.at[k, stage], table.at[k, own], send.at[k, o - 1], recv.at[k, o - 1],
                member, other,
            )

    def gather_wait(k, stage, table, count, source, peer, send, recv):
        for o in range(1, count):
            member, other = peer(o)
            arrived(
                vec_ref.at[k, stage], table.at[k, source(o)], send.at[k, o - 1],
                recv.at[k, o - 1], member, other,
            )
        return jnp.sum(table[k], axis=0)

    def m_to(o):
        return at_m(o), band

    def x_to(o):
        return m, by * across + x_peer(o)

    def y_to(o):
        return m, y_peer(o) * across + bx

    def m_start(k, value):
        gather_start(k, 0, value, allm_ref, members, m, m_to, m_send, m_recv)

    def m_wait(k):
        return gather_wait(k, 0, allm_ref, members, lambda o: at_m(members - o), m_to, m_send, m_recv)

    def x_start(k, value):
        gather_start(k, 1, value, allx_ref, across, bx, x_to, x_send, x_recv)

    def x_wait(k):
        return gather_wait(k, 1, allx_ref, across, lambda o: x_peer(across - o), x_to, x_send, x_recv)

    def y_start(k, value):
        gather_start(k, 2, value, ally_ref, up, by, y_to, y_send, y_recv)

    def y_wait(k):
        return gather_wait(k, 2, ally_ref, up, lambda o: y_peer(up - o), y_to, y_send, y_recv)

    over_tiles(lambda cols: fold(cols, w0_ref[:, cols]))
    smooth(0)
    copies = send_halo(0)

    def first_static(cols, acc):
        value = static_share * mul_wide(krt_ref, w0_ref[:, cols])
        r0s_ref[:, cols] = value
        return acc + squares(value, value)

    zero = jnp.zeros((8, TILE), jnp.float32)
    rr_static = over_tiles(first_static, zero)
    for copy in copies:
        copy.wait_recv()

    def first_members(cols, acc):
        value = mul(t1_ref[...], stacked(0, cols)) * c1_ref[...]
        r0_ref[:, cols] = value
        x_ref[:, cols] = value.astype(jnp.bfloat16)
        return acc + squares(value, value)

    rr_members = over_tiles(first_members, zero)

    smooth(1)
    copies = send_halo(1)
    for copy in copies:
        copy.wait_recv()
    image(1, 0, r0s_ref, im0_ref)

    def weigh(cols, acc):
        value = im0_ref[:, cols]
        weighted = p_ref[:, cols] * value
        gown_ref[:, cols] = weighted.astype(jnp.bfloat16)
        return acc + weighted * value

    q00 = over_tiles(weigh, zero)
    gall_ref[m] = gown_ref[...]
    for o in range(1, members):
        push(gown_ref, gall_ref.at[m], g_send.at[o - 1], g_recv.at[o - 1], at_m(o), band)
    m_start(0, pack([total_of(rr_members + rr_static * (1.0 / members)), total_of(q00)]))
    for o in range(1, members):
        arrived(
            gown_ref, gall_ref.at[at_m(members - o)], g_send.at[o - 1], g_recv.at[o - 1],
            at_m(o), band,
        )

    def gathered(cols):
        return gall_ref[:, :, cols].astype(jnp.float32).reshape(rows2, TILE)

    over_tiles(lambda cols: fold(cols, gathered(cols)))
    x_start(0, m_wait(0))
    smooth(2)
    copies = send_halo(2)

    y_start(0, x_wait(0))

    def second_static(cols):
        field = gathered(cols).astype(jnp.bfloat16)
        r1s_ref[:, cols] = r0s_ref[:, cols] + static_share * (
            mul(krt_ref[0], field) + mul(krt_ref[1], field)
        )

    over_tiles(second_static)
    tot_ref[0] = y_wait(0)
    rr0 = tot_ref[0, 0:1, 0:1]
    q00 = tot_ref[0, 1:2, 0:1]
    alpha0 = rr0 / (rr0 + q00)
    for copy in copies:
        copy.wait_recv()

    def second_residual(cols, acc):
        rr, cross = acc
        first = r0_ref[:, cols]
        hessian = first + mul(t1_ref[...], stacked(2, cols)) * c1_ref[...]
        value = first - alpha0 * hessian
        r1_ref[:, cols] = value
        x_ref[:, cols] = value.astype(jnp.bfloat16)
        return rr + squares(value, value), cross + squares(value, first)

    rr_members, cross_members = over_tiles(second_residual, (zero, zero))
    smooth(3)
    copies = send_halo(3)

    def second_static_residual(cols, acc):
        rr, cross = acc
        first = r0s_ref[:, cols]
        value = first - alpha0 * r1s_ref[:, cols]
        r1s_ref[:, cols] = value
        return rr + squares(value, value), cross + squares(value, first)

    rr_static, cross_static = over_tiles(second_static_residual, (zero, zero))
    for copy in copies:
        copy.wait_recv()
    image(3, 1, r1s_ref, im1_ref)

    def second_sums(cols, acc):
        q11, q01 = acc
        value = im1_ref[:, cols]
        weighted = p_ref[:, cols] * value
        return q11 + weighted * value, q01 + weighted * im0_ref[:, cols]

    q11, q01 = over_tiles(second_sums, (zero, zero))
    share = 1.0 / members
    m_start(1, pack([
        total_of(rr_members + rr_static * share),
        total_of(cross_members + cross_static * share),
        total_of(q11),
        total_of(q01),
    ]))
    x_start(1, m_wait(1))
    y_start(1, x_wait(1))
    tot_ref[1] = y_wait(1)
    rr1 = tot_ref[1, 0:1, 0:1]
    cross = tot_ref[1, 1:2, 0:1]
    q11 = tot_ref[1, 2:3, 0:1]
    q01 = tot_ref[1, 3:4, 0:1]
    beta = rr1 / rr0
    length = rr1 + beta * (2.0 * cross + beta * rr0)
    curvature = length + q11 + beta * (2.0 * q01 + beta * q00)
    alpha1 = rr1 / curvature
    ahead = alpha0 + alpha1 * beta

    def finish(cols):
        outm_ref[:, cols] = ahead * r0_ref[:, cols] + alpha1 * r1_ref[:, cols]
        outs_ref[:, cols] = ahead * r0s_ref[:, cols] + alpha1 * r1s_ref[:, cols]
        inc_ref[:, cols] = ahead * im0_ref[:, cols] + alpha1 * im1_ref[:, cols]

    over_tiles(finish)
    for copy in sends:
        copy.wait_send()


def shards(ensemble, member_weight, member_of_slot, halfwidth, static_root, innovation, precision):
    f32, bf16 = jnp.float32, jnp.bfloat16
    _, slots, levels, rows, width = ensemble.shape
    members = lax.axis_size("member")
    bands = lax.axis_size("band")
    band = lax.axis_index("band")
    me = lax.axis_index("member")
    across = 4 if bands % 4 == 0 else 1
    up = bands // across
    padded = -(-width // TILE) * TILE
    tiles = padded // TILE
    eight = slots * rows
    rows1, rows2 = levels * rows, levels * eight

    def flat(field):
        field = jnp.transpose(field, (1, 0, 2, 3))
        field = jnp.pad(field, ((0, 0), (0, 0), (0, 0), (0, padded - width)))
        return field.reshape(rows2, padded)

    picker = member_of_slot == jnp.arange(members, dtype=jnp.int32)
    scaled = jnp.sum(jnp.where(picker, member_weight, 0.0))
    precise = precision.astype(f32)
    ens = flat(ensemble[0].astype(f32) * scaled)
    w0 = flat(innovation.astype(f32) * precise[None])
    own = lax.dynamic_slice_in_dim(precise, me, 1, 0)[0]
    own = jnp.pad(jnp.concatenate([own] * slots, axis=0), ((0, 0), (0, padded - width)))

    lev1 = np.repeat(np.arange(levels), rows)
    row1 = np.tile(np.arange(rows), levels)
    lev2 = np.repeat(np.arange(levels), eight)
    row2 = np.tile(np.arange(rows), levels * slots)
    lev3 = np.tile(lev1, 3)
    row3 = np.concatenate([row1 - rows, row1, row1 + rows])
    side = np.repeat(np.arange(3), rows1)
    spans = halfwidth.astype(f32) + 1.0
    inside = jnp.where(
        side == 0, band > 0, jnp.where(side == 2, band < bands - 1, True)
    )

    def taper(lev, row):
        span = jnp.repeat(spans, len(lev) // levels)[:, None]
        offsets = np.abs(row3[None, :] - row[:, None]).astype(np.float32)
        same = lev[:, None] == lev3[None, :]
        weights = jnp.maximum(span - offsets, 0.0)
        weights = jnp.where(same & inside[None, :], weights, 0.0).astype(bf16)
        return weights, ensemble_share / (span * span)

    t1, c1 = taper(lev1, row1)
    t2, c2 = taper(lev2, row2)
    slot2 = np.tile(np.repeat(np.arange(slots), rows), levels)
    same12 = (row1[:, None] == row2[None, :]).astype(np.float32)
    sel = jnp.asarray(
        same12 * (lev1[:, None] == lev2[None, :]) * (slot2[None, :] == 0), bf16
    )
    krt = jnp.repeat(jnp.repeat(static_root.T, rows, 0), eight, 1) * same12
    root_row = lax.dynamic_slice_in_dim(static_root, me, 1, 0)
    rowe = np.tile(np.arange(rows), slots)
    krm = jnp.repeat(root_row, rows, 1) * (rowe[:, None] == row1[None, :])
    weights = jnp.asarray(window_weights(width, padded), bf16)

    vmem = pl.BlockSpec(memory_space=pltpu.VMEM)
    dma = pltpu.SemaphoreType.DMA
    outm, outs, inc = pl.pallas_call(
        functools.partial(kernel, members, bands, across, tiles),
        out_shape=[
            jax.ShapeDtypeStruct((rows1, padded), f32),
            jax.ShapeDtypeStruct((rows1, padded), f32),
            jax.ShapeDtypeStruct((eight, padded), f32),
        ],
        in_specs=[vmem] * 11,
        out_specs=[vmem] * 3,
        scratch_shapes=[
            pltpu.VMEM((rows1, padded), bf16),
            pltpu.VMEM((4, rows1, padded), bf16),
            pltpu.VMEM((4, rows1, padded), bf16),
            pltpu.VMEM((4, rows1, padded), bf16),
            pltpu.VMEM((2, levels, eight, padded), bf16),
            pltpu.VMEM((2, members - 1, eight, padded), bf16),
            pltpu.VMEM((eight, padded), bf16),
            pltpu.VMEM((levels, eight, padded), bf16),
            pltpu.VMEM((rows1, padded), f32),
            pltpu.VMEM((rows1, padded), f32),
            pltpu.VMEM((rows1, padded), f32),
            pltpu.VMEM((rows1, padded), f32),
            pltpu.VMEM((eight, padded), f32),
            pltpu.VMEM((eight, padded), f32),
            pltpu.VMEM((2, 3, 8, 128), f32),
            pltpu.VMEM((2, 8, 128), f32),
            pltpu.VMEM((2, members, 8, 128), f32),
            pltpu.VMEM((2, across, 8, 128), f32),
            pltpu.VMEM((2, up, 8, 128), f32),
            dma((4, 2)),
            dma((4, 2)),
            dma((2, members - 1)),
            dma((2, members - 1)),
            dma((members - 1,)),
            dma((members - 1,)),
            dma((2, members - 1)),
            dma((2, members - 1)),
            dma((2, max(across - 1, 1))),
            dma((2, max(across - 1, 1))),
            dma((2, max(up - 1, 1))),
            dma((2, max(up - 1, 1))),
        ],
        compiler_params=pltpu.CompilerParams(collective_id=0, has_side_effects=True),
    )(ens, w0, own, t1, t2, c1, c2, sel, halves(krt), halves(krm), weights)
    control = outm[:, :width].reshape(1, levels, rows, width)
    static = outs[:, :width].reshape(levels, rows, width)
    increment = inc[:, :width].reshape(slots, 1, rows, width)
    return control, static, increment


def solution(mesh):
    return jax.shard_map(
        shards,
        mesh=mesh,
        in_specs=(
            P("member", None, None, "band", None),
            P(),
            P("member"),
            P(),
            P(),
            P(None, None, "band", None),
            P(None, "band", None),
        ),
        out_specs=(
            P("member", None, "band", None),
            P(None, "band", None),
            P(None, "member", "band", None),
        ),
        check_vma=False,
    )
```

time: 659 us -> 124 us (0.19)
  blocking collectives: 298 us -> 0 us
  waiting for transfers between devices: 266 us -> 0 us
  Pallas kernels: 0 us -> 106 us
  starting transfers between devices: 24.4 us -> 0 us
  between operations: 24.5 us -> 1.48 us
  other arithmetic: 23.4 us -> 4.89 us
  matrix products: 8.49 us -> 0 us
    psum x3 -> x0, blocking collectives: 298 us -> none  [the longest x2 196 us: shards(): lax.psum(local_dot(res_members, res_members, res_static, res_static, grou...]
    psum x2 -> x0, waiting for transfers between devices: 243 us -> none  [shards(): summed = lax.psum(partial_image, 'member')]
    pallas_call x0 -> x1, Pallas kernels: none -> 106 us  [shards(): pl.pallas_call(functools.partial(kernel, members, bands, across, tiles),...]
    ppermute x10 -> x0, starting transfers between devices: 24.4 us -> none  [the longest x5 17.9 us: with_halo(): lax.ppermute(lax.slice_in_dim(block, block.shape[dim] - width, None, axis...]
    ppermute x10 -> x0, waiting for transfers between devices: 23.3 us -> none  [the longest x5 18.7 us: with_halo(): lax.ppermute(lax.slice_in_dim(block, 0, width, axis=dim), axis, backward)]
    reduce_sum x11 -> x1, other arithmetic: 12.8 us -> 0.63 us  [shards(): scaled = jnp.sum(jnp.where(picker, member_weight, 0.0))]
    dot_general x10 -> x0, matrix products: 8.49 us -> none  [the longest x5 4.34 us: smooth_longitude(): jnp.einsum('...bm,mo->...bo', window, kernel, preferred_element_type=jnp....]
  transfers between devices with their start and end apart: 12 -> 0, of which waited for: 11 -> 0; matrix products, arithmetic and copies ran while one was open for 1% -> 0% of each run, Pallas kernels for 0% -> 0%
where the time goes in v1:
time: 124 us; the launch traced here: 123 us
  Pallas kernels  106 us (85%)
  local copies, waits for them, and re-layouts  11 us (9%)
  other arithmetic  4.89 us (4%)
  between operations  1.48 us (1%)
    pallas_call x1, Pallas kernels, shards(): pl.pallas_call(functools.partial(kernel, members, bands, across, tiles),...  106 us
    unnamed x34, local copies, waits for them, and re-layouts  2.65 us

profile of v1, /device:TPU:1, one launch (start us, length us, event | category | flops | bytes accessed | tf_op | source)
XLA Modules:
  0.0 122.9 jit_solution(4506688044258613106)
XLA Ops:
  1.3 0.6 copy-done.14
  2.0 0.6 fusion.10
  2.7 0.6 copy-done.15
  3.3 0.1 broadcast_in_dim.54
  3.4 0.1 broadcast_in_dim.55
  3.5 0.6 copy-done.11
  4.1 0.6 pad_maximum_fusion.1.krm_ref
  4.7 0.1 broadcast_in_dim.51
  4.9 0.1 sub.29
  5.0 0.1 broadcast_in_dim.48
  5.0 0.1 sub.26
  5.1 0.1 copy.35
  5.3 0.7 div.16.c1_ref
  6.1 0.7 fusion.3.t1_ref
  6.8 0.1 copy-done.6
  7.0 0.6 pad_maximum_fusion.krt_ref
  7.7 0.7 div.17.c2_ref
  8.4 0.7 fusion.1.t2_ref
  9.1 0.6 select_maximum_fusion.p_ref
  9.8 0.3 copy-done.1
  10.1 0.2 multiply_bitcast_fusion
  10.3 0.1 copy.43
  10.4 0.2 pad.12.clone
  10.5 1.2 reshape.78.w0_ref
  11.7 0.8 multiply_bitcast_fusion.1
  12.5 0.1 copy.42
  12.6 0.2 pad.11.clone
  12.7 1.2 reshape.77.ens_ref
  13.9 105.5 %shard_map.184 = (f32[64,1536]{1,0:T(8,128)}, f32[64,1536]{1,0:T(8,128)}, f32[8,1536]{1,0:T(8,128)}) custom-call(f32[128,1536]{1,0:T(8,128)} %reshape.77.ens_ref, f32[128,1536]{1,0:T(8,128)} %reshape.78.w0_ref, f32[8,1536]{1,0:T(8,128)} %select_maximum_fusion.p_ref, bf16[64,192]{1,0:T(8,128)(2,1)} %fusion.3.t1_ref, bf16[128,192]{1,0:T(8,128)(2,1)} %fusion.1.t2_ref, ...), custom_call_target="tpu_custom_call" | custom-call | tf_op jit(solution)/shard_map/pallas_call | solution.py:458
  119.5 1.9 %reshape.81 = f32[1,16,4,1440]{3,2,1,0:T(4,128)} reshape(f32[64,1440]{1,0:T(8,128)} %bitcast.29) | data formatting | bytes 737280 | tf_op jit(solution)/shard_map/reshape | solution.py:502
  121.4 0.9 reshape.82
  122.2 0.6 reshape.83
  (40 shorter events, 0.5 us)
Async XLA Ops:
  0.6 2.0 %copy-start.10 = (f32[16,16]{1,0:T(8,128)S(1)}, f32[16,16]{1,0:T(8,128)}, u32[]{:S(2)}) copy-start(f32[16,16]{1,0:T(8,128)} %param.21) | copy-start | bytes 3076
  1.3 0.7 copy-start.14
  2.0 0.7 copy-start.12
  2.0 0.7 copy-start.13
  2.6 0.7 copy-start.15
  3.4 0.7 copy-start.11
  5.2 0.8 copy-start.5
  5.3 0.8 copy-start.9
  6.1 0.8 copy-start.6
  6.9 1.5 %copy-start.4 = (f32[128,192]{1,0:T(8,128)S(1)}, f32[128,192]{1,0:T(8,128)}, u32[]{:S(2)}) copy-start(f32[128,192]{1,0:T(8,128)} %constant.69) | copy-start | bytes 294916
  7.0 1.4 %copy-start.8 = (pred[128,192]{1,0:T(32,128)(4,1)S(1)}, pred[128,192]{1,0:T(32,128)(4,1)}, u32[]{:S(2)}) copy-start(pred[128,192]{1,0:T(32,128)(4,1)} %constant.53.clone) | copy-start | bytes 73732
  7.0 2.1 %copy-start.3 = (bf16[16,4,1440]{2,1,0:T(4,128)(2,1)S(1)}, bf16[16,4,1440]{2,1,0:T(4,128)(2,1)}, u32[]{:S(2)}) copy-start(bf16[16,4,1440]{2,1,0:T(4,128)(2,1)} %param.23) | copy-start | bytes 552964
  9.1 1.0 copy-start.1
  10.5 1.2 copy-start.2
  119.4 1.9 %copy-start = (f32[64,1536]{1,0:T(8,128)S(1)}, f32[64,1536]{1,0:T(8,128)}, u32[]{:S(2)}) copy-start(f32[64,1536]{1,0:T(8,128)} %get-tuple-element.7) | copy-start | bytes 1179652
  121.4 0.9 copy-start.7

commit v2 on v1

v2 whole, which is shorter than its diff:
```python
import functools
import math

import jax
import jax.numpy as jnp
import numpy as np
from jax import lax
from jax.experimental import pallas as pl
from jax.experimental.pallas import tpu as pltpu
from jax.sharding import PartitionSpec as P

HMAX = 4
LREACH = 18
TILE = 256
EDGE = 128

ensemble_share = 0.8
static_share = 0.6
length_scale = 6.0
MESH = pl.DeviceIdType.MESH


def window_weights(width, padded):
    tiles = padded // TILE
    kinds = []
    for tile in (0, 1, tiles - 1):
        start = tile * TILE
        rows = np.arange(start - EDGE, start + TILE + EDGE)
        if tile == 0:
            rows[:EDGE] = np.arange(padded - EDGE, padded)
        if tile == tiles - 1:
            rows[-EDGE:] = np.arange(EDGE)
        cols = np.arange(start, start + TILE)
        apart = np.abs(rows[:, None] - cols[None, :])
        apart = np.minimum(apart, width - apart)
        near = (apart <= LREACH) & (rows[:, None] < width) & (cols[None, :] < width)
        distance = apart.astype(np.float32)
        values = np.exp(-0.5 * (distance / np.float32(length_scale)) ** 2) / np.float32(
            length_scale * math.sqrt(2.0 * math.pi)
        )
        kinds.append(np.where(near, values, 0.0).astype(np.float32))
    return np.stack(kinds)


def mul(a, b):
    return jnp.dot(a, b, preferred_element_type=jnp.float32)


def mul_wide(weights, field):
    high = field.astype(jnp.bfloat16)
    low = (field - high.astype(jnp.float32)).astype(jnp.bfloat16)
    return mul(weights[0], high) + mul(weights[0], low) + mul(weights[1], high)


def kernel(
    members, bands, across, tiles, groups,
    weight_ref, slot_ref, half_ref,
    ens_ref, w0_ref, p_ref, root_ref, wk_ref,
    outm_ref, outs_ref, inc_ref,
    t1_ref, t2_ref, c1_ref, c2_ref, sel_ref, krt_ref, krm_ref,
    x_ref, s_ref, hp_ref, hn_ref, part_ref, rs_ref, gown_ref, gall_ref,
    r0_ref, r1_ref, r0s_ref, r1s_ref, im0_ref, im1_ref,
    vec_ref, tot_ref, allm_ref, allx_ref, ally_ref,
    h_send, h_recv, rs_send, rs_recv, g_send, g_recv, m_send, m_recv, x_send, x_recv, y_send, y_recv,
):
    f32, bf16 = jnp.float32, jnp.bfloat16
    m = lax.axis_index("member")
    band = lax.axis_index("band")
    up = bands // across
    by = band // across
    bx = lax.rem(band, across)
    levels, eight = gall_ref.shape[0], gall_ref.shape[1]
    rows = eight // 2
    rows1, rows2 = levels * rows, levels * eight
    each = levels // groups
    small, large = each * rows, each * eight
    my_group = lax.rem(m, groups)
    my_place = m // groups

    def at_m(o):
        return lax.rem(m + o, members)

    def at_band(o):
        return lax.rem(band + o, bands)

    def x_peer(o):
        return lax.rem(bx + o, across)

    def y_peer(o):
        return lax.rem(by + o, up)

    def place(level):
        return lax.rem(level, groups) * each + level // groups

    barrier = pltpu.get_barrier_semaphore()
    greeted = 0
    for o in range(1, members):
        pl.semaphore_signal(
            barrier, inc=1, device_id=(at_m(o), band), device_id_type=MESH
        )
        greeted += 1
    others = [at_band(1), at_band(bands - 1)]
    others += [by * across + x_peer(o) for o in range(1, across)]
    others += [y_peer(o) * across + bx for o in range(1, up)]
    for other in others:
        pl.semaphore_signal(barrier, inc=1, device_id=(m, other), device_id_type=MESH)
        greeted += 1

    def iota(shape, axis):
        return lax.broadcasted_iota(jnp.int32, shape, axis)

    def over(index, size):
        return lax.shift_right_logical(index, size.bit_length() - 1)

    def level_of(index, height):
        inside = index & (each * height - 1)
        return over(inside, height) * groups + over(index, each * height)

    def span_of(level):
        span = jnp.zeros(level.shape, jnp.int32)
        for at in range(levels):
            span = jnp.where(level == at, half_ref[at] + 1, span)
        return span

    low_side = jnp.where(band > 0, 1, 0)
    high_side = jnp.where(band < bands - 1, 1, 0)
    scaled = jnp.float32(0.0)
    for at in range(members):
        scaled = scaled + jnp.where(slot_ref[0] == at, weight_ref[at], 0.0)

    def taper(height, out, factors, extra):
        shape = (levels * height, 3 * small)
        line, col = iota(shape, 0), iota(shape, 1)
        side = jnp.where(col >= small, 1, 0) + jnp.where(col >= 2 * small, 1, 0)
        within = col - side * small
        apart = jnp.abs((within & (rows - 1)) + (side - 1) * rows - (line & (rows - 1)))
        same = over(within, rows) == over(line & (each * height - 1), height)
        seen = jnp.where(side == 0, low_side, jnp.where(side == 2, high_side, 1)) == 1
        span = span_of(level_of(line, height))
        values = jnp.where(same & seen, jnp.maximum(span - apart, 0), 0)
        out[...] = values.astype(f32).astype(bf16)
        spans = span_of(level_of(iota(factors.shape, 0), height)).astype(f32)
        factors[...] = extra / (spans * spans)

    taper(rows, t1_ref, c1_ref, ensemble_share)
    taper(eight, t2_ref, c2_ref, ensemble_share * scaled)

    def ones(condition):
        return jnp.where(condition, 1.0, 0.0).astype(f32)

    line, col = iota((small, large), 0), iota((small, large), 1)
    picked = over(line, rows) * eight + (line & (rows - 1))
    sel_ref[...] = ones(col == picked).astype(bf16)
    shape = (rows1, levels)
    place1 = ones(level_of(iota(shape, 0), rows) == iota(shape, 1)).astype(bf16)
    shape = (levels, rows2)
    level2 = ones(level_of(iota(shape, 1), eight) == iota(shape, 0)).astype(bf16)
    shape = (levels, rows1)
    level1 = ones(level_of(iota(shape, 1), rows) == iota(shape, 0)).astype(bf16)
    shape = (eight, levels)
    mine = ones(iota(shape, 1) == m).astype(bf16)
    shape = (rows1, rows2)
    match = ones((iota(shape, 0) & (rows - 1)) == (iota(shape, 1) & (rows - 1)))
    shape = (eight, rows1)
    match_row = ones((iota(shape, 0) & (rows - 1)) == (iota(shape, 1) & (rows - 1)))
    root = root_ref[...]
    root_high = root.astype(bf16)
    root_low = (root - root_high.astype(f32)).astype(bf16)
    for at, piece in enumerate((root_high, root_low)):
        spread = lax.dot_general(
            place1, piece, (((1,), (1,)), ((), ())), preferred_element_type=f32
        )
        krt_ref[at] = (mul(spread.astype(bf16), level2) * match).astype(bf16)
        spread = mul(mine, piece)
        krm_ref[at] = (mul(spread.astype(bf16), level1) * match_row).astype(bf16)

    sends = []

    def push(src, dst, send, recv, member, other):
        copy = pltpu.make_async_remote_copy(
            src_ref=src, dst_ref=dst, send_sem=send, recv_sem=recv,
            device_id=(member, other), device_id_type=MESH,
        )
        copy.start()
        sends.append(copy)
        return copy

    def arrived(like, dst, send, recv, member, other):
        pltpu.make_async_remote_copy(
            src_ref=like, dst_ref=dst, send_sem=send, recv_sem=recv,
            device_id=(member, other), device_id_type=MESH,
        ).wait_recv()

    def columns(i):
        return pl.ds(pl.multiple_of(i * TILE, TILE), TILE)

    def over_tiles(body, init=None):
        if init is None:
            def step(i, carry):
                body(columns(i))
                return carry
            lax.fori_loop(0, tiles, step, 0)
            return None
        return lax.fori_loop(0, tiles, lambda i, carry: body(columns(i), carry), init)

    every = [slice(i * TILE, (i + 1) * TILE) for i in range(tiles)]
    last = tiles * TILE

    def smooth(phase, g):
        for i, cols in enumerate(every):
            start, stop = i * TILE - EDGE, (i + 1) * TILE + EDGE
            if i == 0:
                window = jnp.concatenate([x_ref[g, :, last - EDGE :], x_ref[g, :, :stop]], axis=1)
            elif i == tiles - 1:
                window = jnp.concatenate([x_ref[g, :, start:], x_ref[g, :, :EDGE]], axis=1)
            else:
                window = x_ref[g, :, start:stop]
            kind = 0 if i == 0 else 2 if i == tiles - 1 else 1
            s_ref[phase, g, :, cols] = mul(window, wk_ref[kind]).astype(bf16)

    def send_halo(phase, g):
        return (
            push(
                s_ref.at[phase, g], hp_ref.at[phase, g], h_send.at[phase, g, 0],
                h_recv.at[phase, g, 0], m, at_band(1),
            ),
            push(
                s_ref.at[phase, g], hn_ref.at[phase, g], h_send.at[phase, g, 1],
                h_recv.at[phase, g, 1], m, at_band(bands - 1),
            ),
        )

    def small_of(g):
        return slice(g * small, (g + 1) * small)

    def large_of(g):
        return slice(g * large, (g + 1) * large)

    def stacked(phase, g, cols):
        return jnp.concatenate(
            [hp_ref[phase, g, :, cols], s_ref[phase, g, :, cols], hn_ref[phase, g, :, cols]],
            axis=0,
        )

    def fold(g, field):
        for cols in every:
            products = (ens_ref[large_of(g), cols] * field(g, cols)).reshape(each, eight, TILE)
            both = (products + pltpu.roll(products, rows, 1)) * scaled
            both = both.reshape(large, TILE).astype(bf16)
            x_ref[g, :, cols] = mul(sel_ref[...], both).astype(bf16)

    def squares(a, b):
        product = a * b
        return jnp.sum(product.reshape(product.shape[0] // 8, 8, TILE), axis=0)

    def image(phase, stage, static_ref, out, halos):
        def static(cols):
            out[:, cols] = static_share * mul_wide(krm_ref, static_ref[:, cols])

        over_tiles(static)
        for g in range(groups):
            for copy in halos[g]:
                copy.wait_recv()
            for cols in every:
                localized = mul(t2_ref[large_of(g)], stacked(phase, g, cols))
                products = localized * c2_ref[large_of(g), 0:1] * ens_ref[large_of(g), cols]
                part_ref[stage, g * each : (g + 1) * each, :, cols] = products.reshape(
                    each, eight, TILE
                ).astype(bf16)
            for o in range(each):
                there = lax.rem(my_place + o, each)
                copy = pltpu.make_async_remote_copy(
                    src_ref=part_ref.at[stage, g * each + there], dst_ref=rs_ref.at[stage, m],
                    send_sem=rs_send.at[stage, g * each + o], recv_sem=rs_recv.at[stage, m],
                    device_id=(there * groups + g, band), device_id_type=MESH,
                )
                if o > 0:
                    copy.start()
                    sends.append(copy)
                else:
                    pl.when(my_group != g)(copy.start)
                    later.append((my_group != g, copy))
        rs_ref[stage, m] = part_ref[stage, place(m)]
        for o in range(1, members):
            source = at_m(members - o)
            arrived(
                part_ref.at[stage, 0], rs_ref.at[stage, source], rs_send.at[stage, 0],
                rs_recv.at[stage, source], at_m(o), band,
            )

        def collect(cols):
            out[:, cols] = out[:, cols] + jnp.sum(rs_ref[stage, :, :, cols].astype(f32), axis=0)

        over_tiles(collect)

    later = []

    def total_of(acc):
        return jnp.sum(jnp.sum(acc, axis=1, keepdims=True), axis=0, keepdims=True)

    def pack(values):
        line = iota((8, 128), 0)
        packed = jnp.zeros((8, 128), f32)
        for at, value in enumerate(values):
            packed = jnp.where(line == at, value, packed)
        return packed

    def gather_start(k, stage, value, table, count, own, peer, send, recv):
        vec_ref[k, stage] = value
        table[k, own] = value
        for o in range(1, count):
            member, other = peer(o)
            push(
                vec_ref.at[k, stage], table.at[k, own], send.at[k, o - 1], recv.at[k, o - 1],
                member, other,
            )

    def gather_wait(k, stage, table, count, source, peer, send, recv):
        for o in range(1, count):
            member, other = peer(o)
            arrived(
                vec_ref.at[k, stage], table.at[k, source(o)], send.at[k, o - 1],
                recv.at[k, o - 1], member, other,
            )
        return jnp.sum(table[k], axis=0)

    def m_to(o):
        return at_m(o), band

    def x_to(o):
        return m, by * across + x_peer(o)

    def y_to(o):
        return m, y_peer(o) * across + bx

    def m_start(k, value):
        gather_start(k, 0, value, allm_ref, members, m, m_to, m_send, m_recv)

    def m_wait(k):
        return gather_wait(k, 0, allm_ref, members, lambda o: at_m(members - o), m_to, m_send, m_recv)

    def x_start(k, value):
        gather_start(k, 1, value, allx_ref, across, bx, x_to, x_send, x_recv)

    def x_wait(k):
        return gather_wait(k, 1, allx_ref, across, lambda o: x_peer(across - o), x_to, x_send, x_recv)

    def y_start(k, value):
        gather_start(k, 2, value, ally_ref, up, by, y_to, y_send, y_recv)

    def y_wait(k):
        return gather_wait(k, 2, ally_ref, up, lambda o: y_peer(up - o), y_to, y_send, y_recv)

    halos = []
    for g in range(groups):
        fold(g, lambda g, cols: w0_ref[large_of(g), cols])
        smooth(0, g)
        if g == 0:
            pl.semaphore_wait(barrier, greeted)
        halos.append(send_halo(0, g))

    def first_static(cols, acc):
        value = static_share * mul_wide(krt_ref, w0_ref[:, cols])
        r0s_ref[:, cols] = value
        return acc + squares(value, value)

    zero = jnp.zeros((8, TILE), f32)
    rr_static = over_tiles(first_static, zero)

    rr_members = zero
    waits, halos = halos, []
    for g in range(groups):
        for copy in waits[g]:
            copy.wait_recv()
        for cols in every:
            value = mul(t1_ref[small_of(g)], stacked(0, g, cols)) * c1_ref[small_of(g), 0:1]
            r0_ref[small_of(g), cols] = value
            x_ref[g, :, cols] = value.astype(bf16)
            rr_members = rr_members + squares(value, value)
        smooth(1, g)
        halos.append(send_halo(1, g))
    image(1, 0, r0s_ref, im0_ref, halos)

    def weigh(cols, acc):
        value = im0_ref[:, cols]
        weighted = p_ref[:, cols] * value
        gown_ref[:, cols] = weighted.astype(bf16)
        return acc + weighted * value

    q00 = over_tiles(weigh, zero)
    gall_ref[place(m)] = gown_ref[...]
    for o in range(1, members):
        push(
            gown_ref, gall_ref.at[place(m)], g_send.at[o - 1], g_recv.at[m], at_m(o), band
        )
    m_start(0, pack([total_of(rr_members + rr_static * (1.0 / members)), total_of(q00)]))
    for o in range(1, members):
        source = at_m(members - o)
        arrived(
            gown_ref, gall_ref.at[place(source)], g_send.at[o - 1], g_recv.at[source],
            at_m(o), band,
        )

    waits = []
    for g in range(groups):
        fold(g, lambda g, cols: gall_ref[g * each : (g + 1) * each, :, cols].astype(f32).reshape(
            large, TILE
        ))
        smooth(2, g)
        waits.append(send_halo(2, g))
    x_start(0, m_wait(0))

    def second_static(cols):
        field = gall_ref[:, :, cols].astype(f32).reshape(rows2, TILE).astype(bf16)
        r1s_ref[:, cols] = r0s_ref[:, cols] + static_share * (
            mul(krt_ref[0], field) + mul(krt_ref[1], field)
        )

    over_tiles(second_static)
    y_start(0, x_wait(0))
    tot_ref[0] = y_wait(0)
    rr0 = tot_ref[0, 0:1, 0:1]
    q00 = tot_ref[0, 1:2, 0:1]
    alpha0 = rr0 / (rr0 + q00)
    rr_members = zero
    cross_members = zero
    halos = []
    for g in range(groups):
        for copy in waits[g]:
            copy.wait_recv()
        for cols in every:
            first = r0_ref[small_of(g), cols]
            localized = mul(t1_ref[small_of(g)], stacked(2, g, cols)) * c1_ref[small_of(g), 0:1]
            value = first - alpha0 * (first + localized)
            r1_ref[small_of(g), cols] = value
            x_ref[g, :, cols] = value.astype(bf16)
            rr_members = rr_members + squares(value, value)
            cross_members = cross_members + squares(value, first)
        smooth(3, g)
        halos.append(send_halo(3, g))

    def second_static_residual(cols, acc):
        rr, cross = acc
        first = r0s_ref[:, cols]
        value = first - alpha0 * r1s_ref[:, cols]
        r1s_ref[:, cols] = value
        return rr + squares(value, value), cross + squares(value, first)

    rr_static, cross_static = over_tiles(second_static_residual, (zero, zero))
    image(3, 1, r1s_ref, im1_ref, halos)

    def second_sums(cols, acc):
        q11, q01 = acc
        value = im1_ref[:, cols]
        weighted = p_ref[:, cols] * value
        return q11 + weighted * value, q01 + weighted * im0_ref[:, cols]

    q11, q01 = over_tiles(second_sums, (zero, zero))
    share = 1.0 / members
    m_start(1, pack([
        total_of(rr_members + rr_static * share),
        total_of(cross_members + cross_static * share),
        total_of(q11),
        total_of(q01),
    ]))
    x_start(1, m_wait(1))
    y_start(1, x_wait(1))
    tot_ref[1] = y_wait(1)
    rr1 = tot_ref[1, 0:1, 0:1]
    cross = tot_ref[1, 1:2, 0:1]
    q11 = tot_ref[1, 2:3, 0:1]
    q01 = tot_ref[1, 3:4, 0:1]
    beta = rr1 / rr0
    length = rr1 + beta * (2.0 * cross + beta * rr0)
    curvature = length + q11 + beta * (2.0 * q01 + beta * q00)
    alpha1 = rr1 / curvature
    ahead = alpha0 + alpha1 * beta

    def finish(cols):
        outm_ref[:, cols] = ahead * r0_ref[:, cols] + alpha1 * r1_ref[:, cols]
        outs_ref[:, cols] = ahead * r0s_ref[:, cols] + alpha1 * r1s_ref[:, cols]
        inc_ref[:, cols] = ahead * im0_ref[:, cols] + alpha1 * im1_ref[:, cols]

    over_tiles(finish)
    for copy in sends:
        copy.wait_send()
    for sent, copy in later:
        pl.when(sent)(copy.wait_send)


def shards(ensemble, member_weight, member_of_slot, halfwidth, static_root, innovation, precision):
    f32, bf16 = jnp.float32, jnp.bfloat16
    _, slots, levels, rows, width = ensemble.shape
    members = lax.axis_size("member")
    bands = lax.axis_size("band")
    me = lax.axis_index("member")
    across = 4 if bands % 4 == 0 else 1
    up = bands // across
    groups = max(levels // 4, 1)
    each = levels // groups
    padded = -(-width // TILE) * TILE
    tiles = padded // TILE
    eight = slots * rows
    rows1, rows2 = levels * rows, levels * eight
    small, large = each * rows, each * eight

    def flat(field):
        field = field.reshape(slots, each, groups, rows, width)
        field = jnp.transpose(field, (2, 1, 0, 3, 4))
        field = jnp.pad(field, ((0, 0),) * 4 + ((0, padded - width),))
        return field.reshape(rows2, padded)

    precise = precision.astype(f32)
    ens = flat(ensemble[0].astype(f32))
    w0 = flat(innovation.astype(f32) * precise[None])
    own = lax.dynamic_slice_in_dim(precise, me, 1, 0)[0]
    own = jnp.pad(jnp.concatenate([own] * slots, axis=0), ((0, 0), (0, padded - width)))
    weights = jnp.asarray(window_weights(width, padded), bf16)

    vmem = pl.BlockSpec(memory_space=pltpu.VMEM)
    smem = pl.BlockSpec(memory_space=pltpu.SMEM)
    dma = pltpu.SemaphoreType.DMA
    outm, outs, inc = pl.pallas_call(
        functools.partial(kernel, members, bands, across, tiles, groups),
        out_shape=[
            jax.ShapeDtypeStruct((rows1, padded), f32),
            jax.ShapeDtypeStruct((rows1, padded), f32),
            jax.ShapeDtypeStruct((eight, padded), f32),
        ],
        in_specs=[smem] * 3 + [vmem] * 5,
        out_specs=[vmem] * 3,
        scratch_shapes=[
            pltpu.VMEM((rows1, 3 * small), bf16),
            pltpu.VMEM((rows2, 3 * small), bf16),
            pltpu.VMEM((rows1, 128), f32),
            pltpu.VMEM((rows2, 128), f32),
            pltpu.VMEM((small, large), bf16),
            pltpu.VMEM((2, rows1, rows2), bf16),
            pltpu.VMEM((2, eight, rows1), bf16),
            pltpu.VMEM((groups, small, padded), bf16),
            pltpu.VMEM((4, groups, small, padded), bf16),
            pltpu.VMEM((4, groups, small, padded), bf16),
            pltpu.VMEM((4, groups, small, padded), bf16),
            pltpu.VMEM((2, levels, eight, padded), bf16),
            pltpu.VMEM((2, members, eight, padded), bf16),
            pltpu.VMEM((eight, padded), bf16),
            pltpu.VMEM((levels, eight, padded), bf16),
            pltpu.VMEM((rows1, padded), f32),
            pltpu.VMEM((rows1, padded), f32),
            pltpu.VMEM((rows1, padded), f32),
            pltpu.VMEM((rows1, padded), f32),
            pltpu.VMEM((eight, padded), f32),
            pltpu.VMEM((eight, padded), f32),
            pltpu.VMEM((2, 3, 8, 128), f32),
            pltpu.VMEM((2, 8, 128), f32),
            pltpu.VMEM((2, members, 8, 128), f32),
            pltpu.VMEM((2, across, 8, 128), f32),
            pltpu.VMEM((2, up, 8, 128), f32),
            dma((4, groups, 2)),
            dma((4, groups, 2)),
            dma((2, members)),
            dma((2, members)),
            dma((members,)),
            dma((members,)),
            dma((2, members - 1)),
            dma((2, members - 1)),
            dma((2, max(across - 1, 1))),
            dma((2, max(across - 1, 1))),
            dma((2, max(up - 1, 1))),
            dma((2, max(up - 1, 1))),
        ],
        compiler_params=pltpu.CompilerParams(collective_id=0, has_side_effects=True),
    )(member_weight, member_of_slot, halfwidth, ens, w0, own, static_root, weights)

    def unflat(field):
        field = field[:, :width].reshape(groups, each, rows, width)
        return jnp.transpose(field, (1, 0, 2, 3)).reshape(levels, rows, width)

    increment = inc[:, :width].reshape(slots, 1, rows, width)
    return unflat(outm)[None], unflat(outs), increment


def solution(mesh):
    return jax.shard_map(
        shards,
        mesh=mesh,
        in_specs=(
            P("member", None, None, "band", None),
            P(),
            P("member"),
            P(),
            P(),
            P(None, None, "band", None),
            P(None, "band", None),
        ),
        out_specs=(
            P("member", None, "band", None),
            P(None, "band", None),
            P(None, "member", "band", None),
        ),
        check_vma=False,
    )
```

time: 124 us -> 98.9 us (0.80)
  Pallas kernels: 106 us -> 88.8 us
  local copies, waits for them, and re-layouts: 11 us -> 6.51 us
  other arithmetic: 4.89 us -> 1.87 us
    pallas_call x1, Pallas kernels: 106 us -> 88.8 us  [shards(): pl.pallas_call(functools.partial(kernel, members, bands, across, tiles, g...]
    unnamed x34 -> x8, local copies, waits for them, and re-layouts: 2.65 us -> 0.39 us
    reshape x3, local copies, waits for them, and re-layouts: 2.82 us -> 1.3 us  [the longest x2 1.22 us: unflat(): field = field[:, :width].reshape(groups, each, rows, width)]
    transpose x1 -> x2, local copies, waits for them, and re-layouts: 0.07 us -> 1.54 us  [unflat(): return jnp.transpose(field, (1, 0, 2, 3)).reshape(levels, rows, width)]
    div x2 -> x0, local copies, waits for them, and re-layouts: 1.41 us -> none  [taper(): return (weights, ensemble_share / (span * span))]
    convert_element_type x2 -> x0, other arithmetic: 1.41 us -> none  [taper(): weights = jnp.where(same & inside[None, :], weights, 0.0).astype(bf16)]
where the time goes in v2:
time: 98.9 us; the launch traced here: 98.6 us
  Pallas kernels  88.8 us (90%)
  local copies, waits for them, and re-layouts  6.51 us (7%)
  other arithmetic  1.87 us (2%)
  between operations  1.44 us (1%)
    pallas_call x1, Pallas kernels, shards(): pl.pallas_call(functools.partial(kernel, members, bands, across, tiles, g...  88.8 us
    reshape x2, local copies, waits for them, and re-layouts, flat(): return field.reshape(rows2, padded)  2.33 us

profile of v2, /device:TPU:1, one launch (start us, length us, event | category | flops | bytes accessed | tf_op | source)
XLA Modules:
  0.0 98.6 jit_solution(4224703740082291755)
XLA Ops:
  0.6 0.0 copy-start
  1.3 1.0 convert_element_type.18
  2.3 0.6 select_maximum_fusion.p_ref
  3.0 0.0 copy-done
  3.0 0.1 copy.19
  3.1 0.2 pad_convert_fusion
  3.3 0.0 copy-start.2
  3.3 1.2 %reshape.43.ens_ref = f32[128,1536]{1,0:T(8,128)} reshape(f32[4,4,2,4,1536]{4,3,2,1,0:T(4,128)S(1)} %pad_convert_fusion) | data formatting | bytes 1572864 | tf_op jit(solution)/shard_map/reshape | solution.py:511
  4.5 0.0 copy-done.2
  4.5 0.1 convert_multiply_fusion
  4.6 0.1 copy.18
  4.7 0.2 pad.13
  4.8 1.2 %reshape.37.w0_ref = f32[128,1536]{1,0:T(8,128)} reshape(f32[4,4,2,4,1536]{4,3,2,1,0:T(4,128)S(1)} %pad.13) | data formatting | bytes 1572864 | tf_op jit(solution)/shard_map/reshape | solution.py:511
  6.0 88.8 %shard_map.103 = (f32[64,1536]{1,0:T(8,128)}, f32[64,1536]{1,0:T(8,128)}, f32[8,1536]{1,0:T(8,128)}) custom-call(f32[16]{0:T(128)} %weight_ref.1, s32[1]{0:T(128)S(6)} %copy.20.slot_ref, s32[16]{0:T(128)} %half_ref.1, f32[128,1536]{1,0:T(8,128)} %reshape.43.ens_ref, f32[128,1536]{1,0:T(8,128)} %reshape.37.w0_ref, f32[8,1536]{1,0:T(8,128)} %select_maximum_fusion.p_ref, ...), custom_call_target="tpu_custom_call" | custom-call | tf_op jit(solution)/shard_map/pallas_call | solution.py:523
  94.8 1.1 %reshape.38 = f32[4,4,4,1440]{3,2,1,0:T(4,128)S(1)} reshape(f32[64,1440]{1,0:T(8,128)} %bitcast.31) | data formatting | bytes 737280 | tf_op jit(solution)/shard_map/reshape | solution.py:576
  95.9 0.0 copy-start.1
  95.9 0.8 copy.13
  96.7 0.4 copy-done.1
  97.1 0.1 reshape.39
  97.2 0.0 copy-start.3
  97.2 0.8 copy.14
  98.0 0.0 copy-done.3
  98.0 0.6 reshape.41
  (1 shorter events, 0.0 us)
Async XLA Ops:
  0.6 2.3 %copy-start = (bf16[1,2,16,4,1440]{4,3,2,1,0:T(4,128)(2,1)S(1)}, bf16[1,2,16,4,1440]{4,3,2,1,0:T(4,128)(2,1)}, u32[]{:S(2)}) copy-start(bf16[1,2,16,4,1440]{4,3,2,1,0:T(4,128)(2,1)} %param.8) | copy-start | bytes 1105924
  3.3 1.2 %copy-start.2 = (bf16[2,16,4,1440]{3,2,1,0:T(4,128)(2,1)S(1)}, bf16[2,16,4,1440]{3,2,1,0:T(4,128)(2,1)}, u32[]{:S(2)}) copy-start(bf16[2,16,4,1440]{3,2,1,0:T(4,128)(2,1)} %param.13) | copy-start | bytes 1105924
  95.9 1.1 %copy-start.1 = (f32[64,1536]{1,0:T(8,128)S(1)}, f32[64,1536]{1,0:T(8,128)}, u32[]{:S(2)}) copy-start(f32[64,1536]{1,0:T(8,128)} %get-tuple-element.7) | copy-start | bytes 1179652
  97.2 0.8 copy-start.3

commit v3 on v2

--- a/solution.py
+++ b/solution.py
@@ -58,10 +58,10 @@
     ens_ref, w0_ref, p_ref, root_ref, wk_ref,
     outm_ref, outs_ref, inc_ref,
     t1_ref, t2_ref, c1_ref, c2_ref, sel_ref, krt_ref, krm_ref,
-    x_ref, s_ref, hp_ref, hn_ref, part_ref, rs_ref, gown_ref, gall_ref,
+    x_ref, s_ref, hp_ref, hn_ref, part_ref, pair_ref, sum_ref, rs_ref, gown_ref, gall_ref,
     r0_ref, r1_ref, r0s_ref, r1s_ref, im0_ref, im1_ref,
     vec_ref, tot_ref, allm_ref, allx_ref, ally_ref,
-    h_send, h_recv, rs_send, rs_recv, g_send, g_recv, m_send, m_recv, x_send, x_recv, y_send, y_recv,
+    h_send, h_recv, pair_send, pair_recv, rs_send, rs_recv, g_send, g_recv, m_send, m_recv, x_send, x_recv, y_send, y_recv,
 ):
     f32, bf16 = jnp.float32, jnp.bfloat16
     m = lax.axis_index("member")
@@ -74,6 +74,10 @@
     rows1, rows2 = levels * rows, levels * eight
     each = levels // groups
     small, large = each * rows, each * eight
+    chips = members // 2
+    core = lax.rem(m, 2)
+    chip = m // 2
+    partner = m + 1 - 2 * core
     my_group = lax.rem(m, groups)
     my_place = m // groups
 
@@ -253,6 +257,49 @@
         product = a * b
         return jnp.sum(product.reshape(product.shape[0] // 8, 8, TILE), axis=0)
 
+    def pair_copy(stage, g):
+        return pltpu.make_async_remote_copy(
+            src_ref=part_ref.at[stage, g * each : (g + 1) * each],
+            dst_ref=pair_ref.at[stage, g],
+            send_sem=pair_send.at[stage, g], recv_sem=pair_recv.at[stage, g],
+            device_id=(partner, band), device_id_type=MESH,
+        )
+
+    def sum_copy(stage, g, o):
+        there = lax.rem(my_place + o, each)
+        return pltpu.make_async_remote_copy(
+            src_ref=sum_ref.at[stage, g * each + there], dst_ref=rs_ref.at[stage, chip],
+            send_sem=rs_send.at[stage, g * each + o], recv_sem=rs_recv.at[stage, chip],
+            device_id=(there * groups + g, band), device_id_type=MESH,
+        )
+
+    def forward(stage, g):
+        @pl.when(core == g % 2)
+        def _():
+            pair_copy(stage, g).wait_recv()
+            span = slice(g * each, (g + 1) * each)
+            for cols in every:
+                sum_ref[stage, span, :, cols] = (
+                    part_ref[stage, span, :, cols].astype(f32)
+                    + pair_ref[stage, g, :, :, cols].astype(f32)
+                ).astype(bf16)
+            for o in range(1, each):
+                sum_copy(stage, g, o).start()
+            pl.when(my_group != g)(sum_copy(stage, g, 0).start)
+
+            @pl.when(my_group == g)
+            def _():
+                rs_ref[stage, chip] = sum_ref[stage, place(m)]
+
+    def settle(stage, g):
+        pl.when(core != g % 2)(pair_copy(stage, g).wait_send)
+
+        @pl.when(core == g % 2)
+        def _():
+            for o in range(1, each):
+                sum_copy(stage, g, o).wait_send()
+            pl.when(my_group != g)(sum_copy(stage, g, 0).wait_send)
+
     def image(phase, stage, static_ref, out, halos):
         def static(cols):
             out[:, cols] = static_share * mul_wide(krm_ref, static_ref[:, cols])
@@ -267,33 +314,21 @@
                 part_ref[stage, g * each : (g + 1) * each, :, cols] = products.reshape(
                     each, eight, TILE
                 ).astype(bf16)
-            for o in range(each):
-                there = lax.rem(my_place + o, each)
-                copy = pltpu.make_async_remote_copy(
-                    src_ref=part_ref.at[stage, g * each + there], dst_ref=rs_ref.at[stage, m],
-                    send_sem=rs_send.at[stage, g * each + o], recv_sem=rs_recv.at[stage, m],
-                    device_id=(there * groups + g, band), device_id_type=MESH,
-                )
-                if o > 0:
-                    copy.start()
-                    sends.append(copy)
-                else:
-                    pl.when(my_group != g)(copy.start)
-                    later.append((my_group != g, copy))
-        rs_ref[stage, m] = part_ref[stage, place(m)]
-        for o in range(1, members):
-            source = at_m(members - o)
+            if g > 0:
+                forward(stage, g - 1)
+            pl.when(core != g % 2)(pair_copy(stage, g).start)
+        forward(stage, groups - 1)
+        for o in range(1, chips):
+            source = lax.rem(chip + chips - o, chips)
             arrived(
-                part_ref.at[stage, 0], rs_ref.at[stage, source], rs_send.at[stage, 0],
-                rs_recv.at[stage, source], at_m(o), band,
+                sum_ref.at[stage, 0], rs_ref.at[stage, source], rs_send.at[stage, 0],
+                rs_recv.at[stage, source], at_m(2 * o), band,
             )
 
         def collect(cols):
             out[:, cols] = out[:, cols] + jnp.sum(rs_ref[stage, :, :, cols].astype(f32), axis=0)
 
         over_tiles(collect)
-
-    later = []
 
     def total_of(acc):
         return jnp.sum(jnp.sum(acc, axis=1, keepdims=True), axis=0, keepdims=True)
@@ -389,17 +424,22 @@
 
     q00 = over_tiles(weigh, zero)
     gall_ref[place(m)] = gown_ref[...]
-    for o in range(1, members):
-        push(
-            gown_ref, gall_ref.at[place(m)], g_send.at[o - 1], g_recv.at[m], at_m(o), band
-        )
     m_start(0, pack([total_of(rr_members + rr_static * (1.0 / members)), total_of(q00)]))
-    for o in range(1, members):
-        source = at_m(members - o)
-        arrived(
-            gown_ref, gall_ref.at[place(source)], g_send.at[o - 1], g_recv.at[source],
-            at_m(o), band,
-        )
+    order = sorted(range(1, chips), key=lambda o: min(o, chips - o))
+    for o in order[::-1]:
+        push(gown_ref, gall_ref.at[place(m)], g_send.at[o], g_recv.at[m], at_m(2 * o), band)
+    push(gown_ref, gall_ref.at[place(m)], g_send.at[0], g_recv.at[m], partner, band)
+    x_start(0, m_wait(0))
+    for o in order:
+        source = at_m(members - 2 * o)
+        spot = gall_ref.at[place(source)]
+        arrived(gown_ref, spot, g_send.at[o], g_recv.at[source], at_m(2 * o), band)
+        push(spot, spot, g_send.at[chips + o], g_recv.at[source], partner, band)
+    y_start(0, x_wait(0))
+    for o in [0] + order:
+        source = lax.rem(partner + members - 2 * o, members)
+        spot = gall_ref.at[place(source)]
+        arrived(gown_ref, spot, g_send.at[0], g_recv.at[source], partner, band)
 
     waits = []
     for g in range(groups):
@@ -408,7 +448,6 @@
         ))
         smooth(2, g)
         waits.append(send_halo(2, g))
-    x_start(0, m_wait(0))
 
     def second_static(cols):
         field = gall_ref[:, :, cols].astype(f32).reshape(rows2, TILE).astype(bf16)
@@ -417,7 +456,6 @@
         )
 
     over_tiles(second_static)
-    y_start(0, x_wait(0))
     tot_ref[0] = y_wait(0)
     rr0 = tot_ref[0, 0:1, 0:1]
     q00 = tot_ref[0, 1:2, 0:1]
@@ -484,8 +522,9 @@
     over_tiles(finish)
     for copy in sends:
         copy.wait_send()
-    for sent, copy in later:
-        pl.when(sent)(copy.wait_send)
+    for stage in range(2):
+        for g in range(groups):
+            settle(stage, g)
 
 
 def shards(ensemble, member_weight, member_of_slot, halfwidth, static_root, innovation, precision):
@@ -542,7 +581,9 @@
             pltpu.VMEM((4, groups, small, padded), bf16),
             pltpu.VMEM((4, groups, small, padded), bf16),
             pltpu.VMEM((2, levels, eight, padded), bf16),
-            pltpu.VMEM((2, members, eight, padded), bf16),
+            pltpu.VMEM((2, groups, each, eight, padded), bf16),
+            pltpu.VMEM((2, levels, eight, padded), bf16),
+            pltpu.VMEM((2, members // 2, eight, padded), bf16),
             pltpu.VMEM((eight, padded), bf16),
             pltpu.VMEM((levels, eight, padded), bf16),
             pltpu.VMEM((rows1, padded), f32),
@@ -558,8 +599,10 @@
             pltpu.VMEM((2, up, 8, 128), f32),
             dma((4, groups, 2)),
             dma((4, groups, 2)),
+            dma((2, groups)),
+            dma((2, groups)),
             dma((2, members)),
-            dma((2, members)),
+            dma((2, members // 2)),
             dma((members,)),
             dma((members,)),
             dma((2, members - 1)),

time: 98.9 us -> 90.5 us (0.915)
  Pallas kernels: 88.8 us -> 80.3 us
    pallas_call x1, Pallas kernels: 88.8 us -> 80.3 us  [shards(): pl.pallas_call(functools.partial(kernel, members, bands, across, tiles, g...]
where the time goes in v3:
time: 90.5 us; the launch traced here: 90.1 us
  Pallas kernels  80.3 us (89%)
  local copies, waits for them, and re-layouts  6.51 us (7%)
  other arithmetic  1.87 us (2%)
  between operations  1.44 us (2%)
    pallas_call x1, Pallas kernels, shards(): pl.pallas_call(functools.partial(kernel, members, bands, across, tiles, g...  80.3 us
    reshape x2, local copies, waits for them, and re-layouts, flat(): return field.reshape(rows2, padded)  2.33 us

profile of v3, /device:TPU:1, one launch (start us, length us, event | category | flops | bytes accessed | tf_op | source)
XLA Modules:
  0.0 90.1 jit_solution(14920230466713170208)
XLA Ops:
  0.6 0.0 copy-start
  1.3 1.0 %convert_element_type.18 = f32[16,4,1440]{2,1,0:T(4,128)S(1)} convert(bf16[16,4,1440]{2,1,0:T(4,128)(2,1)} %param.14) | non-fusion elementwise | flops 92160 | bytes 552960 | tf_op jit(solution)/shard_map/convert_element_type | solution.py:552
  2.3 0.6 select_maximum_fusion.p_ref
  3.0 0.0 copy-done
  3.0 0.1 copy.19
  3.1 0.2 pad_convert_fusion
  3.3 0.0 copy-start.2
  3.3 1.2 %reshape.43.ens_ref = f32[128,1536]{1,0:T(8,128)} reshape(f32[4,4,2,4,1536]{4,3,2,1,0:T(4,128)S(1)} %pad_convert_fusion) | data formatting | bytes 1572864 | tf_op jit(solution)/shard_map/reshape | solution.py:550
  4.5 0.0 copy-done.2
  4.5 0.1 convert_multiply_fusion
  4.6 0.1 copy.18
  4.7 0.2 pad.13
  4.8 1.2 %reshape.37.w0_ref = f32[128,1536]{1,0:T(8,128)} reshape(f32[4,4,2,4,1536]{4,3,2,1,0:T(4,128)S(1)} %pad.13) | data formatting | bytes 1572864 | tf_op jit(solution)/shard_map/reshape | solution.py:550
  6.0 80.3 %shard_map.103 = (f32[64,1536]{1,0:T(8,128)}, f32[64,1536]{1,0:T(8,128)}, f32[8,1536]{1,0:T(8,128)}) custom-call(f32[16]{0:T(128)} %weight_ref.1, s32[1]{0:T(128)S(6)} %copy.20.slot_ref, s32[16]{0:T(128)} %half_ref.1, f32[128,1536]{1,0:T(8,128)} %reshape.43.ens_ref, f32[128,1536]{1,0:T(8,128)} %reshape.37.w0_ref, f32[8,1536]{1,0:T(8,128)} %select_maximum_fusion.p_ref, ...), custom_call_target="tpu_custom_call" | custom-call | tf_op jit(solution)/shard_map/pallas_call | solution.py:562
  86.3 1.1 %reshape.38 = f32[4,4,4,1440]{3,2,1,0:T(4,128)S(1)} reshape(f32[64,1440]{1,0:T(8,128)} %bitcast.31) | data formatting | bytes 737280 | tf_op jit(solution)/shard_map/reshape | solution.py:619
  87.4 0.0 copy-start.1
  87.4 0.8 copy.13
  88.2 0.4 copy-done.1
  88.6 0.1 reshape.39
  88.7 0.0 copy-start.3
  88.7 0.8 copy.14
  89.5 0.0 copy-done.3
  89.5 0.6 reshape.41
  (1 shorter events, 0.0 us)
Async XLA Ops:
  0.6 2.3 %copy-start = (bf16[1,2,16,4,1440]{4,3,2,1,0:T(4,128)(2,1)S(1)}, bf16[1,2,16,4,1440]{4,3,2,1,0:T(4,128)(2,1)}, u32[]{:S(2)}) copy-start(bf16[1,2,16,4,1440]{4,3,2,1,0:T(4,128)(2,1)} %param.8) | copy-start | bytes 1105924
  3.3 1.2 %copy-start.2 = (bf16[2,16,4,1440]{3,2,1,0:T(4,128)(2,1)S(1)}, bf16[2,16,4,1440]{3,2,1,0:T(4,128)(2,1)}, u32[]{:S(2)}) copy-start(bf16[2,16,4,1440]{3,2,1,0:T(4,128)(2,1)} %param.13) | copy-start | bytes 1105924
  87.4 1.1 %copy-start.1 = (f32[64,1536]{1,0:T(8,128)S(1)}, f32[64,1536]{1,0:T(8,128)}, u32[]{:S(2)}) copy-start(f32[64,1536]{1,0:T(8,128)} %get-tuple-element.7) | copy-start | bytes 1179652
  88.7 0.8 copy-start.3

commit v4 on v3

--- a/solution.py
+++ b/solution.py
@@ -55,8 +55,9 @@
 def kernel(
     members, bands, across, tiles, groups,
     weight_ref, slot_ref, half_ref,
-    ens_ref, w0_ref, p_ref, root_ref, wk_ref,
+    raw_ref, innov_ref, prec_ref, root_ref, wk_ref,
     outm_ref, outs_ref, inc_ref,
+    ens_ref, w0_ref, p_ref,
     t1_ref, t2_ref, c1_ref, c2_ref, sel_ref, krt_ref, krm_ref,
     x_ref, s_ref, hp_ref, hn_ref, part_ref, pair_ref, sum_ref, rs_ref, gown_ref, gall_ref,
     r0_ref, r1_ref, r0s_ref, r1s_ref, im0_ref, im1_ref,
@@ -178,6 +179,24 @@
         spread = mul(mine, piece)
         krm_ref[at] = (mul(spread.astype(bf16), level1) * match_row).astype(bf16)
 
+    width = prec_ref.shape[2]
+    for target in (ens_ref, w0_ref, p_ref):
+        target[:, width - width % 128 :] = jnp.zeros(
+            (target.shape[0], target.shape[1] - width + width % 128), f32
+        )
+
+    def load(g):
+        for j in range(each):
+            level = j * groups + g
+            lines = slice((g * each + j) * eight, (g * each + j + 1) * eight)
+            precise = prec_ref[level].astype(f32)
+            ens_ref[lines, :width] = jnp.concatenate(
+                [raw_ref[0, t, level].astype(f32) for t in range(2)], axis=0
+            )
+            w0_ref[lines, :width] = jnp.concatenate(
+                [innov_ref[t, level].astype(f32) * precise for t in range(2)], axis=0
+            )
+
     sends = []
 
     def push(src, dst, send, recv, member, other):
@@ -388,6 +407,7 @@
 
     halos = []
     for g in range(groups):
+        load(g)
         fold(g, lambda g, cols: w0_ref[large_of(g), cols])
         smooth(0, g)
         if g == 0:
@@ -399,6 +419,8 @@
         r0s_ref[:, cols] = value
         return acc + squares(value, value)
 
+    precise = prec_ref[m].astype(f32)
+    p_ref[:, :width] = jnp.concatenate([precise, precise], axis=0)
     zero = jnp.zeros((8, TILE), f32)
     rr_static = over_tiles(first_static, zero)
 
@@ -514,12 +536,21 @@
     alpha1 = rr1 / curvature
     ahead = alpha0 + alpha1 * beta
 
-    def finish(cols):
-        outm_ref[:, cols] = ahead * r0_ref[:, cols] + alpha1 * r1_ref[:, cols]
-        outs_ref[:, cols] = ahead * r0s_ref[:, cols] + alpha1 * r1s_ref[:, cols]
-        inc_ref[:, cols] = ahead * im0_ref[:, cols] + alpha1 * im1_ref[:, cols]
-
-    over_tiles(finish)
+    def blend(first, second, lines):
+        return ahead * first[lines, :width] + alpha1 * second[lines, :width]
+
+    for start in range(0, rows1, eight):
+        lines = slice(start, start + eight)
+        members_out = blend(r0_ref, r1_ref, lines)
+        static_out = blend(r0s_ref, r1s_ref, lines)
+        for at in range(2):
+            line = start // rows + at
+            level = line % each * groups + line // each
+            outm_ref[0, level] = members_out[at * rows : (at + 1) * rows]
+            outs_ref[level] = static_out[at * rows : (at + 1) * rows]
+    increment = blend(im0_ref, im1_ref, slice(0, eight))
+    for t in range(2):
+        inc_ref[t, 0] = increment[t * rows : (t + 1) * rows]
     for copy in sends:
         copy.wait_send()
     for stage in range(2):
@@ -532,7 +563,6 @@
     _, slots, levels, rows, width = ensemble.shape
     members = lax.axis_size("member")
     bands = lax.axis_size("band")
-    me = lax.axis_index("member")
     across = 4 if bands % 4 == 0 else 1
     up = bands // across
     groups = max(levels // 4, 1)
@@ -543,32 +573,24 @@
     rows1, rows2 = levels * rows, levels * eight
     small, large = each * rows, each * eight
 
-    def flat(field):
-        field = field.reshape(slots, each, groups, rows, width)
-        field = jnp.transpose(field, (2, 1, 0, 3, 4))
-        field = jnp.pad(field, ((0, 0),) * 4 + ((0, padded - width),))
-        return field.reshape(rows2, padded)
-
-    precise = precision.astype(f32)
-    ens = flat(ensemble[0].astype(f32))
-    w0 = flat(innovation.astype(f32) * precise[None])
-    own = lax.dynamic_slice_in_dim(precise, me, 1, 0)[0]
-    own = jnp.pad(jnp.concatenate([own] * slots, axis=0), ((0, 0), (0, padded - width)))
     weights = jnp.asarray(window_weights(width, padded), bf16)
 
     vmem = pl.BlockSpec(memory_space=pltpu.VMEM)
     smem = pl.BlockSpec(memory_space=pltpu.SMEM)
     dma = pltpu.SemaphoreType.DMA
-    outm, outs, inc = pl.pallas_call(
+    return pl.pallas_call(
         functools.partial(kernel, members, bands, across, tiles, groups),
         out_shape=[
-            jax.ShapeDtypeStruct((rows1, padded), f32),
-            jax.ShapeDtypeStruct((rows1, padded), f32),
-            jax.ShapeDtypeStruct((eight, padded), f32),
+            jax.ShapeDtypeStruct((1, levels, rows, width), f32),
+            jax.ShapeDtypeStruct((levels, rows, width), f32),
+            jax.ShapeDtypeStruct((slots, 1, rows, width), f32),
         ],
         in_specs=[smem] * 3 + [vmem] * 5,
         out_specs=[vmem] * 3,
         scratch_shapes=[
+            pltpu.VMEM((rows2, padded), f32),
+            pltpu.VMEM((rows2, padded), f32),
+            pltpu.VMEM((eight, padded), f32),
             pltpu.VMEM((rows1, 3 * small), bf16),
             pltpu.VMEM((rows2, 3 * small), bf16),
             pltpu.VMEM((rows1, 128), f32),
@@ -613,14 +635,10 @@
             dma((2, max(up - 1, 1))),
         ],
         compiler_params=pltpu.CompilerParams(collective_id=0, has_side_effects=True),
-    )(member_weight, member_of_slot, halfwidth, ens, w0, own, static_root, weights)
-
-    def unflat(field):
-        field = field[:, :width].reshape(groups, each, rows, width)
-        return jnp.transpose(field, (1, 0, 2, 3)).reshape(levels, rows, width)
-
-    increment = inc[:, :width].reshape(slots, 1, rows, width)
-    return unflat(outm)[None], unflat(outs), increment
+    )(
+        member_weight, member_of_slot, halfwidth, ensemble, innovation, precision,
+        static_root, weights,
+    )
 
 
 def solution(mesh):

time: 90.5 us -> 84.7 us (0.936)
  local copies, waits for them, and re-layouts: 6.51 us -> 3.24 us
  other arithmetic: 1.87 us -> 0 us
    reshape x6 -> x0, local copies, waits for them, and re-layouts: 4.27 us -> none  [the longest x2 2.33 us: flat(): return field.reshape(rows2, padded)]
    unnamed x8 -> x7, local copies, waits for them, and re-layouts: 0.39 us -> 3.24 us
    transpose x2 -> x0, local copies, waits for them, and re-layouts: 1.54 us -> none  [unflat(): return jnp.transpose(field, (1, 0, 2, 3)).reshape(levels, rows, width)]
    convert_element_type x1 -> x0, other arithmetic: 0.95 us -> none  [shards(): precise = precision.astype(f32)]
where the time goes in v4:
time: 84.7 us; the launch traced here: 84.5 us
  Pallas kernels  80 us (94%)
  local copies, waits for them, and re-layouts  3.24 us (4%)
  between operations  1.3 us (2%)
    pallas_call x1, Pallas kernels, shards(): pl.pallas_call(functools.partial(kernel, members, bands, across, tiles, g...  80 us
    unnamed x7, local copies, waits for them, and re-layouts  3.24 us

profile of v4, /device:TPU:1, one launch (start us, length us, event | category | flops | bytes accessed | tf_op | source)
XLA Modules:
  0.0 84.5 jit_solution(12146966535701058681)
XLA Ops:
  1.3 80.0 %shard_map.103 = (f32[1,16,4,1440]{3,2,1,0:T(4,128)}, f32[16,4,1440]{2,1,0:T(4,128)}, f32[2,1,4,1440]{3,2,1,0:T(4,128)}) custom-call(f32[16]{0:T(128)} %weight_ref.1, s32[1]{0:T(128)S(6)} %copy.14.slot_ref, s32[16]{0:T(128)} %half_ref.1, bf16[1,2,16,4,1440]{4,3,2,1,0:T(4,128)(2,1)} %raw_ref.1, bf16[2,16,4,1440]{3,2,1,0:T(4,128)(2,1)} %innov_ref.1, ...), custom_call_target="tpu_custom_call" | custom-call | tf_op jit(solution)/shard_map/pallas_call | solution.py:581
  81.3 0.0 copy-start
  81.3 1.8 %copy.15 = f32[1,16,4,1440]{3,2,1,0:T(4,128)} copy(f32[1,16,4,1440]{3,2,1,0:T(4,128)} %get-tuple-element.6) | data formatting | bytes 737280
  83.1 0.0 copy-done
  83.1 0.0 copy-start.1
  83.1 0.7 copy.16
  83.8 0.1 copy-done.1
  83.9 0.6 copy.17
Async XLA Ops:
  81.3 1.8 %copy-start = (f32[16,4,1440]{2,1,0:T(4,128)S(1)}, f32[16,4,1440]{2,1,0:T(4,128)}, u32[]{:S(2)}) copy-start(f32[16,4,1440]{2,1,0:T(4,128)} %get-tuple-element.7) | copy-start | bytes 1105924
  83.1 0.8 copy-start.1

commit v5 on v4

--- a/solution.py
+++ b/solution.py
@@ -53,23 +53,21 @@
 
 
 def kernel(
-    members, bands, across, tiles, groups,
+    members, bands, tiles, groups,
     weight_ref, slot_ref, half_ref,
-    raw_ref, innov_ref, prec_ref, root_ref, wk_ref,
+    raw_hbm, innov_hbm, prec_hbm, root_hbm, wk_hbm,
     outm_ref, outs_ref, inc_ref,
+    raw_ref, innov_ref, prec_ref, root_ref, wk_ref, in_sem,
     ens_ref, w0_ref, p_ref,
     t1_ref, t2_ref, c1_ref, c2_ref, sel_ref, krt_ref, krm_ref,
     x_ref, s_ref, hp_ref, hn_ref, part_ref, pair_ref, sum_ref, rs_ref, gown_ref, gall_ref,
     r0_ref, r1_ref, r0s_ref, r1s_ref, im0_ref, im1_ref,
-    vec_ref, tot_ref, allm_ref, allx_ref, ally_ref,
-    h_send, h_recv, pair_send, pair_recv, rs_send, rs_recv, g_send, g_recv, m_send, m_recv, x_send, x_recv, y_send, y_recv,
+    vec_ref, tot_ref, allm_ref, allb_ref,
+    h_send, h_recv, pair_send, pair_recv, rs_send, rs_recv, g_send, g_recv, m_send, m_recv, b_send, b_recv,
 ):
     f32, bf16 = jnp.float32, jnp.bfloat16
     m = lax.axis_index("member")
     band = lax.axis_index("band")
-    up = bands // across
-    by = band // across
-    bx = lax.rem(band, across)
     levels, eight = gall_ref.shape[0], gall_ref.shape[1]
     rows = eight // 2
     rows1, rows2 = levels * rows, levels * eight
@@ -88,15 +86,18 @@
     def at_band(o):
         return lax.rem(band + o, bands)
 
-    def x_peer(o):
-        return lax.rem(bx + o, across)
-
-    def y_peer(o):
-        return lax.rem(by + o, up)
-
     def place(level):
         return lax.rem(level, groups) * each + level // groups
 
+    fetches = [
+        pltpu.make_async_copy(src, dst, in_sem.at[at])
+        for at, (src, dst) in enumerate([
+            (root_hbm, root_ref), (raw_hbm, raw_ref), (innov_hbm, innov_ref),
+            (prec_hbm, prec_ref), (wk_hbm, wk_ref),
+        ])
+    ]
+    for fetch in fetches:
+        fetch.start()
     barrier = pltpu.get_barrier_semaphore()
     greeted = 0
     for o in range(1, members):
@@ -104,9 +105,7 @@
             barrier, inc=1, device_id=(at_m(o), band), device_id_type=MESH
         )
         greeted += 1
-    others = [at_band(1), at_band(bands - 1)]
-    others += [by * across + x_peer(o) for o in range(1, across)]
-    others += [y_peer(o) * across + bx for o in range(1, up)]
+    others = [at_band(o) for o in range(1, bands)]
     for other in others:
         pl.semaphore_signal(barrier, inc=1, device_id=(m, other), device_id_type=MESH)
         greeted += 1
@@ -168,6 +167,9 @@
     match = ones((iota(shape, 0) & (rows - 1)) == (iota(shape, 1) & (rows - 1)))
     shape = (eight, rows1)
     match_row = ones((iota(shape, 0) & (rows - 1)) == (iota(shape, 1) & (rows - 1)))
+    for fetch in fetches:
+        fetch.wait()
+
     root = root_ref[...]
     root_high = root.astype(bf16)
     root_low = (root - root_high.astype(f32)).astype(bf16)
@@ -381,11 +383,8 @@
     def m_to(o):
         return at_m(o), band
 
-    def x_to(o):
-        return m, by * across + x_peer(o)
-
-    def y_to(o):
-        return m, y_peer(o) * across + bx
+    def b_to(o):
+        return m, at_band(o)
 
     def m_start(k, value):
         gather_start(k, 0, value, allm_ref, members, m, m_to, m_send, m_recv)
@@ -393,17 +392,13 @@
     def m_wait(k):
         return gather_wait(k, 0, allm_ref, members, lambda o: at_m(members - o), m_to, m_send, m_recv)
 
-    def x_start(k, value):
-        gather_start(k, 1, value, allx_ref, across, bx, x_to, x_send, x_recv)
-
-    def x_wait(k):
-        return gather_wait(k, 1, allx_ref, across, lambda o: x_peer(across - o), x_to, x_send, x_recv)
-
-    def y_start(k, value):
-        gather_start(k, 2, value, ally_ref, up, by, y_to, y_send, y_recv)
-
-    def y_wait(k):
-        return gather_wait(k, 2, ally_ref, up, lambda o: y_peer(up - o), y_to, y_send, y_recv)
+    def b_start(k, value):
+        gather_start(k, 1, value, allb_ref, bands, band, b_to, b_send, b_recv)
+
+    def b_wait(k):
+        return gather_wait(
+            k, 1, allb_ref, bands, lambda o: at_band(bands - o), b_to, b_send, b_recv
+        )
 
     halos = []
     for g in range(groups):
@@ -451,13 +446,12 @@
     for o in order[::-1]:
         push(gown_ref, gall_ref.at[place(m)], g_send.at[o], g_recv.at[m], at_m(2 * o), band)
     push(gown_ref, gall_ref.at[place(m)], g_send.at[0], g_recv.at[m], partner, band)
-    x_start(0, m_wait(0))
+    b_start(0, m_wait(0))
     for o in order:
         source = at_m(members - 2 * o)
         spot = gall_ref.at[place(source)]
         arrived(gown_ref, spot, g_send.at[o], g_recv.at[source], at_m(2 * o), band)
         push(spot, spot, g_send.at[chips + o], g_recv.at[source], partner, band)
-    y_start(0, x_wait(0))
     for o in [0] + order:
         source = lax.rem(partner + members - 2 * o, members)
         spot = gall_ref.at[place(source)]
@@ -478,7 +472,7 @@
         )
 
     over_tiles(second_static)
-    tot_ref[0] = y_wait(0)
+    tot_ref[0] = b_wait(0)
     rr0 = tot_ref[0, 0:1, 0:1]
     q00 = tot_ref[0, 1:2, 0:1]
     alpha0 = rr0 / (rr0 + q00)
@@ -523,9 +517,8 @@
         total_of(q11),
         total_of(q01),
     ]))
-    x_start(1, m_wait(1))
-    y_start(1, x_wait(1))
-    tot_ref[1] = y_wait(1)
+    b_start(1, m_wait(1))
+    tot_ref[1] = b_wait(1)
     rr1 = tot_ref[1, 0:1, 0:1]
     cross = tot_ref[1, 1:2, 0:1]
     q11 = tot_ref[1, 2:3, 0:1]
@@ -563,8 +556,6 @@
     _, slots, levels, rows, width = ensemble.shape
     members = lax.axis_size("member")
     bands = lax.axis_size("band")
-    across = 4 if bands % 4 == 0 else 1
-    up = bands // across
     groups = max(levels // 4, 1)
     each = levels // groups
     padded = -(-width // TILE) * TILE
@@ -579,15 +570,21 @@
     smem = pl.BlockSpec(memory_space=pltpu.SMEM)
     dma = pltpu.SemaphoreType.DMA
     return pl.pallas_call(
-        functools.partial(kernel, members, bands, across, tiles, groups),
+        functools.partial(kernel, members, bands, tiles, groups),
         out_shape=[
             jax.ShapeDtypeStruct((1, levels, rows, width), f32),
             jax.ShapeDtypeStruct((levels, rows, width), f32),
             jax.ShapeDtypeStruct((slots, 1, rows, width), f32),
         ],
-        in_specs=[smem] * 3 + [vmem] * 5,
+        in_specs=[smem] * 3 + [pl.BlockSpec(memory_space=pltpu.HBM)] * 5,
         out_specs=[vmem] * 3,
         scratch_shapes=[
+            pltpu.VMEM(ensemble.shape, bf16),
+            pltpu.VMEM(innovation.shape, bf16),
+            pltpu.VMEM(precision.shape, bf16),
+            pltpu.VMEM(static_root.shape, f32),
+            pltpu.VMEM(weights.shape, bf16),
+            dma((5,)),
             pltpu.VMEM((rows2, padded), f32),
             pltpu.VMEM((rows2, padded), f32),
             pltpu.VMEM((eight, padded), f32),
@@ -614,11 +611,10 @@
             pltpu.VMEM((rows1, padded), f32),
             pltpu.VMEM((eight, padded), f32),
             pltpu.VMEM((eight, padded), f32),
-            pltpu.VMEM((2, 3, 8, 128), f32),
+            pltpu.VMEM((2, 2, 8, 128), f32),
             pltpu.VMEM((2, 8, 128), f32),
             pltpu.VMEM((2, members, 8, 128), f32),
-            pltpu.VMEM((2, across, 8, 128), f32),
-            pltpu.VMEM((2, up, 8, 128), f32),
+            pltpu.VMEM((2, bands, 8, 128), f32),
             dma((4, groups, 2)),
             dma((4, groups, 2)),
             dma((2, groups)),
@@ -629,10 +625,8 @@
             dma((members,)),
             dma((2, members - 1)),
             dma((2, members - 1)),
-            dma((2, max(across - 1, 1))),
-            dma((2, max(across - 1, 1))),
-            dma((2, max(up - 1, 1))),
-            dma((2, max(up - 1, 1))),
+            dma((2, bands - 1)),
+            dma((2, bands - 1)),
         ],
         compiler_params=pltpu.CompilerParams(collective_id=0, has_side_effects=True),
     )(

time: 84.7 us -> 85 us (level)
  no operation moved by 1% of the time
where the time goes in v5:
time: 85 us; the launch traced here: 84.8 us
  Pallas kernels  80.2 us (94%)
  local copies, waits for them, and re-layouts  3.24 us (4%)
  between operations  1.3 us (2%)
    pallas_call x1, Pallas kernels, shards(): pl.pallas_call(functools.partial(kernel, members, bands, tiles, groups),...  80.2 us
    unnamed x7, local copies, waits for them, and re-layouts  3.24 us

profile of v5, /device:TPU:1, one launch (start us, length us, event | category | flops | bytes accessed | tf_op | source)
XLA Modules:
  0.0 84.8 jit_solution(2466375329110400661)
XLA Ops:
  1.3 80.2 %shard_map.103 = (f32[1,16,4,1440]{3,2,1,0:T(4,128)}, f32[16,4,1440]{2,1,0:T(4,128)}, f32[2,1,4,1440]{3,2,1,0:T(4,128)}) custom-call(f32[16]{0:T(128)} %weight_ref.1, s32[1]{0:T(128)S(6)} %copy.14.slot_ref, s32[16]{0:T(128)} %half_ref.1, bf16[1,2,16,4,1440]{4,3,2,1,0:T(4,128)(2,1)} %raw_hbm.1, bf16[2,16,4,1440]{3,2,1,0:T(4,128)(2,1)} %innov_hbm.1, ...), custom_call_target="tpu_custom_call" | custom-call | tf_op jit(solution)/shard_map/pallas_call | solution.py:572
  81.5 0.0 copy-start
  81.5 1.8 %copy.15 = f32[1,16,4,1440]{3,2,1,0:T(4,128)} copy(f32[1,16,4,1440]{3,2,1,0:T(4,128)} %get-tuple-element.6) | data formatting | bytes 737280
  83.3 0.0 copy-done
  83.3 0.0 copy-start.1
  83.3 0.7 copy.16
  84.1 0.1 copy-done.1
  84.1 0.6 copy.17
Async XLA Ops:
  81.5 1.8 %copy-start = (f32[16,4,1440]{2,1,0:T(4,128)S(1)}, f32[16,4,1440]{2,1,0:T(4,128)}, u32[]{:S(2)}) copy-start(f32[16,4,1440]{2,1,0:T(4,128)} %get-tuple-element.7) | copy-start | bytes 1105924
  83.3 0.8 copy-start.1

commit v6 on v4

--- a/solution.py
+++ b/solution.py
@@ -55,8 +55,9 @@
 def kernel(
     members, bands, across, tiles, groups,
     weight_ref, slot_ref, half_ref,
-    raw_ref, innov_ref, prec_ref, root_ref, wk_ref,
+    raw_hbm, innov_hbm, prec_hbm, root_hbm, wk_hbm,
     outm_ref, outs_ref, inc_ref,
+    raw_ref, innov_ref, prec_ref, root_ref, wk_ref, in_sem,
     ens_ref, w0_ref, p_ref,
     t1_ref, t2_ref, c1_ref, c2_ref, sel_ref, krt_ref, krm_ref,
     x_ref, s_ref, hp_ref, hn_ref, part_ref, pair_ref, sum_ref, rs_ref, gown_ref, gall_ref,
@@ -97,6 +98,15 @@
     def place(level):
         return lax.rem(level, groups) * each + level // groups
 
+    fetches = [
+        pltpu.make_async_copy(src, dst, in_sem.at[at])
+        for at, (src, dst) in enumerate([
+            (root_hbm, root_ref), (raw_hbm, raw_ref), (innov_hbm, innov_ref),
+            (prec_hbm, prec_ref), (wk_hbm, wk_ref),
+        ])
+    ]
+    for fetch in fetches:
+        fetch.start()
     barrier = pltpu.get_barrier_semaphore()
     greeted = 0
     for o in range(1, members):
@@ -168,6 +178,8 @@
     match = ones((iota(shape, 0) & (rows - 1)) == (iota(shape, 1) & (rows - 1)))
     shape = (eight, rows1)
     match_row = ones((iota(shape, 0) & (rows - 1)) == (iota(shape, 1) & (rows - 1)))
+    for fetch in fetches:
+        fetch.wait()
     root = root_ref[...]
     root_high = root.astype(bf16)
     root_low = (root - root_high.astype(f32)).astype(bf16)
@@ -585,9 +597,15 @@
             jax.ShapeDtypeStruct((levels, rows, width), f32),
             jax.ShapeDtypeStruct((slots, 1, rows, width), f32),
         ],
-        in_specs=[smem] * 3 + [vmem] * 5,
+        in_specs=[smem] * 3 + [pl.BlockSpec(memory_space=pltpu.HBM)] * 5,
         out_specs=[vmem] * 3,
         scratch_shapes=[
+            pltpu.VMEM(ensemble.shape, bf16),
+            pltpu.VMEM(innovation.shape, bf16),
+            pltpu.VMEM(precision.shape, bf16),
+            pltpu.VMEM(static_root.shape, f32),
+            pltpu.VMEM(weights.shape, bf16),
+            dma((5,)),
             pltpu.VMEM((rows2, padded), f32),
             pltpu.VMEM((rows2, padded), f32),
             pltpu.VMEM((eight, padded), f32),

time: 84.7 us -> 84 us (level)
  no operation moved by 1% of the time
where the time goes in v6:
time: 84 us; the launch traced here: 83.7 us
  Pallas kernels  79.2 us (94%)
  local copies, waits for them, and re-layouts  3.24 us (4%)
  between operations  1.3 us (2%)
    pallas_call x1, Pallas kernels, shards(): pl.pallas_call(functools.partial(kernel, members, bands, across, tiles, g...  79.2 us
    unnamed x7, local copies, waits for them, and re-layouts  3.24 us

profile of v6, /device:TPU:1, one launch (start us, length us, event | category | flops | bytes accessed | tf_op | source)
XLA Modules:
  0.0 83.7 jit_solution(16224200684273105118)
XLA Ops:
  1.3 79.2 %shard_map.103 = (f32[1,16,4,1440]{3,2,1,0:T(4,128)}, f32[16,4,1440]{2,1,0:T(4,128)}, f32[2,1,4,1440]{3,2,1,0:T(4,128)}) custom-call(f32[16]{0:T(128)} %weight_ref.1, s32[1]{0:T(128)S(6)} %copy.14.slot_ref, s32[16]{0:T(128)} %half_ref.1, bf16[1,2,16,4,1440]{4,3,2,1,0:T(4,128)(2,1)} %raw_hbm.1, bf16[2,16,4,1440]{3,2,1,0:T(4,128)(2,1)} %innov_hbm.1, ...), custom_call_target="tpu_custom_call" | custom-call | tf_op jit(solution)/shard_map/pallas_call | solution.py:593
  80.5 0.0 copy-start
  80.5 1.8 %copy.15 = f32[1,16,4,1440]{3,2,1,0:T(4,128)} copy(f32[1,16,4,1440]{3,2,1,0:T(4,128)} %get-tuple-element.6) | data formatting | bytes 737280
  82.3 0.0 copy-done
  82.3 0.0 copy-start.1
  82.3 0.7 copy.16
  83.0 0.1 copy-done.1
  83.1 0.6 copy.17
Async XLA Ops:
  80.5 1.8 %copy-start = (f32[16,4,1440]{2,1,0:T(4,128)S(1)}, f32[16,4,1440]{2,1,0:T(4,128)}, u32[]{:S(2)}) copy-start(f32[16,4,1440]{2,1,0:T(4,128)} %get-tuple-element.7) | copy-start | bytes 1105924
  82.3 0.8 copy-start.1
